TPU v7x, 256 devices: a whole 4x4x8 slice. The times are simulated.
256 devices in a mesh: fsdp: 8 (over x, core), seq: 32 (over y, z).
Axes of the slice: x: 4, y: 4, z: 8, core: 2. Of those that a mesh axis runs over, the one named last changes fastest.
Arguments:
- tokens: bfloat16 [131072, 2048], P(('fsdp', 'seq')), may hold values from -42 to 42
- qkv_weight: bfloat16 [2048, 3072], P('seq', 'fsdp'), as said below
- out_weight: bfloat16 [1024, 2048], P('seq', 'fsdp'), may hold values from -0.1875 to 0.1875
- adapter_down: bfloat16 [64, 16, 2048], P('seq'), may hold values from -0.125 to 0.125
- adapter_up: bfloat16 [64, 16, 2048], P('seq'), may hold values from -1.5 to 1.5
- lengths: int32 [8, 16], replicated, may hold values from 1 to 1536, 16384 in all within a row
- adapter_ids: int32 [8, 16], replicated, may hold values from 0 to 63
- adapter_slot: int32 [64], replicated, may hold values from 0 to 63, each once
Outputs:
- attn_out: bfloat16 [131072, 2048], P(('fsdp', 'seq'))
Inputs may be any that keep to these rules, and one draw needn't show every extreme that they name: Each row gives the lengths of the 16 requests of one group; a row sums to 16384, and its longest request has exactly 1536 tokens. `adapter_slot`: each slot holds exactly one adapter. `qkv_weight`: entries are of order 1 / sqrt(2048), in some heads' query and key columns up to several times that.
All inputs are finite; a program needn't handle non-finite values.
Results may differ from a plain program's by a relative error of at most 0.023.
Values may be sent and summed in bfloat16 or wider, within the bound.
A program may use at most 128 MiB of HBM per device.

v0:
```python
import jax
import jax.numpy as jnp
from jax import lax
from jax.sharding import PartitionSpec as P

HS = 256
SPAN = 3


eps_norm = 1e-05
adapter_scale_factor = 0.5


def shifted(block, axis, distance):
    devices = range(lax.axis_size(axis))
    route = [(i - distance, i) for i in devices if i - distance in devices]
    return lax.ppermute(block, axis, route)


def layer_norm(token_rows):
    value_vectors = token_rows.astype(jnp.float32)
    average = jnp.mean(value_vectors, axis=-1, keepdims=True)
    centred = value_vectors - average
    variance = jnp.mean(centred * centred, axis=-1, keepdims=True)
    return (centred * lax.rsqrt(variance + eps_norm)).astype(jnp.bfloat16)


def request_info(length_row, position):
    row_ends = jnp.cumsum(length_row)
    request = jnp.sum((position[:, None] >= row_ends[None, :]).astype(jnp.int32), axis=1)
    onehot = (request[:, None] == jnp.arange(length_row.shape[0], dtype=jnp.int32)[None, :]).astype(
        jnp.int32
    )
    begins = jnp.sum(onehot * (row_ends - length_row)[None, :], axis=1)
    return (request, onehot, position - begins)


def rotate(head_rows, position):
    rotary = head_rows.shape[-1] // 4
    halfway = rotary // 2
    inverse = 10000.0 ** (-2.0 * jnp.arange(halfway, dtype=jnp.float32) / rotary)
    angles = position.astype(jnp.float32)[:, None] * inverse[None, :]
    cosine = jnp.cos(angles)[:, None, :]
    sine_part = jnp.sin(angles)[:, None, :]
    leading = head_rows[..., :halfway]
    trailing = head_rows[..., halfway:rotary]
    return jnp.concatenate(
        [
            leading * cosine - trailing * sine_part,
            trailing * cosine + leading * sine_part,
            head_rows[..., rotary:],
        ],
        axis=-1,
    )


def per_device(
    tokens, qkv_weight, out_weight, adapter_down, adapter_up, lengths, adapter_ids, adapter_slot
):
    token_count = tokens.shape[0]
    group_index = lax.axis_index("fsdp")
    block_index = lax.axis_index("seq")
    length_row = lax.dynamic_index_in_dim(lengths, group_index, 0, keepdims=False)
    ids_row = lax.dynamic_index_in_dim(adapter_ids, group_index, 0, keepdims=False)
    position = block_index * token_count + jnp.arange(token_count, dtype=jnp.int32)
    request, onehot, offsets = request_info(length_row, position)
    lookup = (
        ids_row[:, None] == jnp.arange(adapter_slot.shape[0], dtype=jnp.int32)[None, :]
    ).astype(jnp.int32)
    request_slot = jnp.sum(lookup * adapter_slot[None, :], axis=1)
    normed = layer_norm(tokens)
    downs = lax.all_gather(adapter_down, "seq", axis=0, tiled=True)
    ups = lax.all_gather(adapter_up, "seq", axis=0, tiled=True)
    slot_ids = jnp.arange(downs.shape[0], dtype=jnp.int32)
    select = (request_slot[:, None] == slot_ids[None, :]).astype(jnp.bfloat16)
    down_add = jnp.einsum("as,srd->ard", select, downs, preferred_element_type=jnp.float32)
    up_add = jnp.einsum("as,sro->aro", select, ups, preferred_element_type=jnp.float32)
    picked_down = down_add
    picked_up = up_add
    picked_down = picked_down.astype(jnp.bfloat16)
    picked_up = picked_up.astype(jnp.bfloat16)
    ranks = jnp.einsum("td,ard->tar", normed, picked_down, preferred_element_type=jnp.float32)
    ranks = jnp.where(onehot[:, :, None] > 0, ranks, 0.0).astype(jnp.bfloat16)
    adapter_delta = jnp.einsum("tar,aro->to", ranks, picked_up, preferred_element_type=jnp.float32)
    qkv_broad, out_broad = (
        lax.all_gather(qkv_weight, "fsdp", axis=1, tiled=True),
        lax.all_gather(out_weight, "fsdp", axis=1, tiled=True),
    )
    chosen_cols = normed
    query_key_value = jnp.dot(
        chosen_cols,
        lax.all_gather(qkv_broad, "seq", axis=0, tiled=True),
        preferred_element_type=jnp.float32,
    )
    heads_width_total = query_key_value.shape[1] // 3
    head_count = heads_width_total // HS
    query_vectors = (
        query_key_value[:, :heads_width_total]
        + adapter_scale_factor * adapter_delta[:, :heads_width_total]
    )
    keys = query_key_value[:, heads_width_total : 2 * heads_width_total]
    value_vectors = (
        query_key_value[:, 2 * heads_width_total :]
        + adapter_scale_factor * adapter_delta[:, heads_width_total:]
    )
    query_vectors = rotate(query_vectors.reshape(token_count, head_count, HS), offsets).astype(
        jnp.bfloat16
    )
    keys = rotate(keys.reshape(token_count, head_count, HS), offsets).astype(jnp.bfloat16)
    both_parts = jnp.concatenate(
        [keys.reshape(token_count, heads_width_total), value_vectors.astype(jnp.bfloat16)], axis=1
    )
    current = both_parts
    window_list = [both_parts]
    for offset in range(SPAN):
        current = shifted(current, "seq", 1)
        window_list.append(current)
    window = jnp.stack(window_list, axis=0)
    depth = window.shape[0]
    key_position = (
        (block_index - jnp.arange(depth, dtype=jnp.int32))[:, None] * token_count
        + jnp.arange(token_count, dtype=jnp.int32)[None, :]
    ).reshape(-1)
    key_request, key_onehot, key_offsets = request_info(length_row, key_position)
    allowed = (
        (key_request[None, :] == request[:, None])
        & (key_position[None, :] >= 0)
        & (key_position[None, :] <= position[:, None])
    )
    flat_window = window.reshape(depth * token_count, 2 * heads_width_total)
    key_heads = flat_window[:, :heads_width_total].reshape(depth * token_count, head_count, HS)
    value_heads = flat_window[:, heads_width_total:].reshape(depth * token_count, head_count, HS)
    scores = jnp.einsum(
        "qhd,khd->hqk", query_vectors, key_heads, preferred_element_type=jnp.float32
    ) * HS ** (-0.5)
    scores = jnp.where(allowed[None, :, :], scores, -1e30)
    highest = jnp.max(scores, axis=-1, keepdims=True)
    weights = jnp.exp(scores - highest)
    probs = (weights / jnp.sum(weights, axis=-1, keepdims=True)).astype(jnp.bfloat16)
    attended = jnp.einsum("hqk,khd->qhd", probs, value_heads, preferred_element_type=jnp.float32)
    attended = attended.astype(jnp.bfloat16).reshape(token_count, heads_width_total)
    chosen_cols = attended
    mixed = jnp.dot(
        chosen_cols,
        lax.all_gather(out_broad, "seq", axis=0, tiled=True),
        preferred_element_type=jnp.float32,
    )
    return mixed.astype(jnp.bfloat16)


def solution(mesh):
    in_specs = (
        P(("fsdp", "seq"), None),
        P("seq", "fsdp"),
        P("seq", "fsdp"),
        P("seq", None, None),
        P("seq", None, None),
        P(),
        P(),
        P(),
    )
    out_specs = P(("fsdp", "seq"), None)
    return jax.shard_map(
        per_device, mesh=mesh, in_specs=in_specs, out_specs=out_specs, check_vma=False
    )
```

profile of v0, /device:TPU:8, one launch (start us, length us, event | category | flops | bytes accessed | tf_op | source)
XLA Modules:
  0.0 552.4 jit_solution(5145371073915775298)
XLA Ops:
  8.1 14.7 %all_gather.18 = bf16[64,3072]{1,0:T(8,128)(2,1)} all-gather(bf16[64,384]{1,0:T(8,128)(2,1)} %param.9), channel_id=1, replica_groups=mesh['fsdp'=8,'seq'=32] {'fsdp'}, dimensions={1}, use_global_device_ids=true | all-gather | bytes 442368 | tf_op jit(solution)/shard_map/all_gather | solution.py:86
  30.0 63.4 %all-gather.9.cloned.1.call-done = bf16[64,16,2048]{2,1,0:T(8,128)(2,1)} async-done(((bf16[2,16,2048]{2,1,0:T(8,128)(2,1)}), bf16[64,16,2048]{2,1,0:T(8,128)(2,1)}) %all-gather.9.cloned.1.call-update) | async-done | bytes 4194320 | tf_op jit(solution)/shard_map/all_gather | solution.py:73
  93.4 6.7 %fusion.17 = bf16[16,16,2048]{2,0,1:T(8,128)(2,1)S(1)} fusion(bf16[64,16,2048]{2,1,0:T(8,128)(2,1)} %all-gather.9.cloned.1.call-done, s32[16]{0:T(128)S(1)} %select_reduce_fusion.1), kind=kOutput, calls=%fused_computation.24 | convolution fusion | flops 67634176 | bytes 5242944 | tf_op jit(solution)/shard_map/as,sro->aro/dot_general | solution.py:77
  100.1 75.0 %all-gather.7.cloned.1.call-done = bf16[64,16,2048]{2,1,0:T(8,128)(2,1)} async-done(((bf16[2,16,2048]{2,1,0:T(8,128)(2,1)}), bf16[64,16,2048]{2,1,0:T(8,128)(2,1)}) %all-gather.7.cloned.1.call-update) | async-done | bytes 4194320 | tf_op jit(solution)/shard_map/all_gather | solution.py:72
  175.1 7.7 %fusion.14 = bf16[16,16,2048]{2,0,1:T(8,128)(2,1)} fusion(bf16[64,16,2048]{2,1,0:T(8,128)(2,1)} %all-gather.7.cloned.1.call-done, s32[16]{0:T(128)S(1)} %select_reduce_fusion.1), kind=kOutput, calls=%fused_computation.23 | convolution fusion | flops 67634176 | bytes 5242944 | tf_op jit(solution)/shard_map/as,srd->ard/dot_general | solution.py:76
  182.7 5.4 convolution_bitcast_fusion
  188.1 106.5 %all-gather.5.cloned.1.call-done = bf16[2048,3072]{1,0:T(8,128)(2,1)} async-done(((bf16[64,3072]{1,0:T(8,128)(2,1)}), bf16[2048,3072]{1,0:T(8,128)(2,1)}) %all-gather.5.cloned.1.call-update) | async-done | bytes 12582928 | tf_op jit(solution)/shard_map/all_gather | solution.py:92
  294.6 9.9 %fusion.53 = f32[512,3072]{1,0:T(8,128)S(1)} fusion(bf16[2048,3072]{1,0:T(8,128)(2,1)} %all-gather.5.cloned.1.call-done, bf16[512,2048]{1,0:T(8,128)(2,1)S(1)} %copy-done.3, f32[512]{0:T(512)S(1)} %add_rsqrt_fusion, f32[512]{0:T(512)S(1)} %broadcast_multiply_fusion), kind=kOutput, calls=%fused_computation.78 | convolution fusion | flops 6446645248 | bytes 20975616 | tf_op jit(solution)/shard_map/dot_general | solution.py:90
  304.5 3.2 fusion.20
  307.7 2.2 reshape.246
  311.3 2.2 reshape.251
  313.5 2.9 fusion.57
  324.8 49.2 %collective-permute-done = bf16[512,2048]{1,0:T(8,128)(2,1)} collective-permute-done((bf16[512,2048]{1,0:T(8,128)(2,1)S(1)}, bf16[512,2048]{1,0:T(8,128)(2,1)}, u32[]{:S(2)}, u32[]{:S(2)}) %collective-permute-start) | collective-permute-done | bytes 2097184 | tf_op jit(solution)/shard_map/ppermute | solution.py:17
  375.9 14.2 %all_gather.22 = bf16[32,2048]{1,0:T(8,128)(2,1)} all-gather(bf16[32,256]{1,0:T(8,128)(2,1)S(1)} %copy-done.10), channel_id=1, replica_groups=mesh['fsdp'=8,'seq'=32] {'fsdp'}, dimensions={1}, use_global_device_ids=true | all-gather | bytes 147456 | tf_op jit(solution)/shard_map/all_gather | solution.py:87
  390.2 39.0 %collective-permute-done.1 = bf16[512,2048]{1,0:T(8,128)(2,1)} collective-permute-done((bf16[512,2048]{1,0:T(8,128)(2,1)}, bf16[512,2048]{1,0:T(8,128)(2,1)}, u32[]{:S(2)}, u32[]{:S(2)}) %collective-permute-start.1) | collective-permute-done | bytes 2097184 | tf_op jit(solution)/shard_map/ppermute | solution.py:17
  429.1 2.1 collective-permute-start.2
  433.5 64.5 %collective-permute-done.2 = bf16[512,2048]{1,0:T(8,128)(2,1)S(1)} collective-permute-done((bf16[512,2048]{1,0:T(8,128)(2,1)}, bf16[512,2048]{1,0:T(8,128)(2,1)S(1)}, u32[]{:S(2)}, u32[]{:S(2)}) %collective-permute-start.2) | collective-permute-done | bytes 2097184 | tf_op jit(solution)/shard_map/ppermute | solution.py:17
  498.0 3.3 pad_maximum_fusion
  501.4 3.7 fusion.56
  505.1 6.5 %copy.53 = bf16[2048,1024]{0,1:T(8,128)(2,1)} copy(bf16[2048,1024]{1,0:T(8,128)(2,1)} %get-tuple-element.8) | data formatting | bytes 8388608 | tf_op jit(solution)/shard_map/slice | solution.py:132
  511.6 6.5 %copy.62 = bf16[2048,1024]{0,1:T(8,128)(2,1)} copy(bf16[2048,1024]{1,0:T(8,128)(2,1)} %get-tuple-element.7) | data formatting | bytes 8388608
  518.1 11.9 %fusion.59 = (f32[4,512]{1,0:T(4,128)S(1)}, f32[4,512,2048]{2,1,0:T(8,128)}) fusion(pred[512,2048]{1,0:T(8,128)(4,1)S(1)} %compare_and_fusion, bf16[2048,4,256]{0,2,1:T(8,128)(2,1)} %bitcast.52, bf16[512,4,192]{2,0,1:T(8,128)(2,1)S(1)} %copy.91, bf16[512,4,32]{2,0,1:T(8,128)(2,1)S(1)} %copy-done.9, bf16[512,4,32]{2,0,1:T(8,128)(2,1)S(1)} %copy-done.8), kind=kOutput, calls=%fused_computation.83 | convolution fusion | flops 2167408640 | bytes 23076864 | tf_op jit(solution)/shard_map/sub | solution.py:138
  530.0 9.5 %fusion.25 = bf16[4,256,512]{2,1,0:T(8,128)(2,1)S(1)} fusion(bf16[2048,4,256]{0,2,1:T(8,128)(2,1)} %bitcast.51, f32[4,512,2048]{2,1,0:T(8,128)} %get-tuple-element.25, f32[4,512]{1,0:T(4,128)S(1)} %get-tuple-element.24), kind=kOutput, calls=%fused_computation.35 | convolution fusion | flops 2156396544 | bytes 22028288 | tf_op jit(solution)/shard_map/hqk,khd->qhd/dot_general | solution.py:140
  539.6 5.9 %convolution_convert_fusion = bf16[512,2048]{1,0:T(8,128)(2,1)} fusion(bf16[512,1024]{0,1:T(8,128)(2,1)S(1)} %bitcast.58, bf16[1024,2048]{1,0:T(8,128)(2,1)} %all-gather.11.cloned.1.call-done), kind=kOutput, calls=%fused_computation.22 | convolution fusion | flops 2148532224 | bytes 7340032 | tf_op jit(solution)/shard_map/dot_general | solution.py:143
  (66 shorter events, 22.5 us)
Async XLA Ops:
  6.5 17.3 %copy-start = (s32[8,16]{1,0:T(8,128)S(1)}, s32[8,16]{1,0:T(8,128)}, u32[]{:S(2)}) copy-start(s32[8,16]{1,0:T(8,128)} %param.14) | copy-start | bytes 1540
  6.5 21.0 %copy-start.3 = (bf16[512,2048]{1,0:T(8,128)(2,1)S(1)}, bf16[512,2048]{1,0:T(8,128)(2,1)}, u32[]{:S(2)}) copy-start(bf16[512,2048]{1,0:T(8,128)(2,1)} %param.8) | copy-start | bytes 6291460
  6.5 86.9 %all-gather.9.cloned.1.call-start = ((), (), s32[]{:S(2)}) async-start(), calls=%async_computation.2 | async-start | bytes 4325376 | tf_op jit(solution)/shard_map/all_gather | solution.py:73
  7.3 167.8 %all-gather.7.cloned.1.call-start = ((), (), s32[]{:S(2)}) async-start(), calls=%async_computation.1 | async-start | bytes 4325376 | tf_op jit(solution)/shard_map/all_gather | solution.py:72
  8.0 286.6 %all-gather.5.cloned.1.call-start = ((), (), s32[]{:S(2)}) async-start(), calls=%async_computation | async-start | bytes 12976128 | tf_op jit(solution)/shard_map/all_gather | solution.py:92
  22.8 516.7 %all-gather.11.cloned.1.call-start = ((), (), s32[]{:S(2)}) async-start(), calls=%async_computation.3 | async-start | bytes 4325376 | tf_op jit(solution)/shard_map/all_gather | solution.py:145
  294.6 9.9 %copy-start.5 = (f32[512,2048]{1,0:T(8,128)S(1)}, f32[512,2048]{1,0:T(8,128)}, u32[]{:S(2)}) copy-start(f32[512,2048]{1,0:T(8,128)} %convolution_bitcast_fusion) | copy-start | bytes 12582916
  309.9 1.3 copy-start.2
  313.5 2.9 copy-start.7
  318.0 3.0 copy-start.6
  320.8 55.1 %copy-start.10 = (bf16[32,256]{1,0:T(8,128)(2,1)S(1)}, bf16[32,256]{1,0:T(8,128)(2,1)}, u32[]{:S(2)}) copy-start(bf16[32,256]{1,0:T(8,128)(2,1)} %param.10) | copy-start | bytes 49156
  322.9 51.1 %collective-permute-start = (bf16[512,2048]{1,0:T(8,128)(2,1)S(1)}, bf16[512,2048]{1,0:T(8,128)(2,1)}, u32[]{:S(2)}, u32[]{:S(2)}) collective-permute-start(bf16[512,2048]{1,0:T(8,128)(2,1)S(1)} %get-tuple-element.17), channel_id=1, source_target_pairs={{0,1},{1,2},{2,3},{3,4},{4,5},{5,6},{6,7},{7,8},{8,9},{9,10},{10,1... | collective-permute-start | bytes 6291464 | tf_op jit(solution)/shard_map/ppermute | solution.py:17
  374.0 55.1 %collective-permute-start.1 = (bf16[512,2048]{1,0:T(8,128)(2,1)}, bf16[512,2048]{1,0:T(8,128)(2,1)}, u32[]{:S(2)}, u32[]{:S(2)}) collective-permute-start(bf16[512,2048]{1,0:T(8,128)(2,1)} %collective-permute-done), channel_id=1, source_target_pairs={{0,1},{1,2},{2,3},{3,4},{4,5},{5,6},{6,7},{7,8},{8,9},{9,10},{10,1... | collective-permute-start | bytes 6291464 | tf_op jit(solution)/shard_map/ppermute | solution.py:17
  390.1 107.9 %copy-start.4 = (bf16[1,512,2048]{2,1,0:T(8,128)(2,1)S(1)}, bf16[1,512,2048]{2,1,0:T(8,128)(2,1)}, u32[]{:S(2)}) copy-start(bf16[1,512,2048]{2,1,0:T(8,128)(2,1)} %get-tuple-element.16) | copy-start | bytes 6291460
  429.1 68.9 %collective-permute-start.2 = (bf16[512,2048]{1,0:T(8,128)(2,1)}, bf16[512,2048]{1,0:T(8,128)(2,1)S(1)}, u32[]{:S(2)}, u32[]{:S(2)}) collective-permute-start(bf16[512,2048]{1,0:T(8,128)(2,1)} %collective-permute-done.1), channel_id=1, source_target_pairs={{0,1},{1,2},{2,3},{3,4},{4,5},{5,6},{6,7},{7,8},{8,9},{9,10},{10,1... | collective-permute-start | bytes 6291464 | tf_op jit(solution)/shard_map/ppermute | solution.py:17
  511.6 6.5 %copy-start.8 = (bf16[512,4,32]{2,0,1:T(8,128)(2,1)S(1)}, bf16[512,4,32]{2,0,1:T(8,128)(2,1)}, u32[]{:S(2)}) copy-start(bf16[512,4,32]{2,0,1:T(8,128)(2,1)} %get-tuple-element.10) | copy-start | bytes 393220
  511.6 6.5 %copy-start.9 = (bf16[512,4,32]{2,0,1:T(8,128)(2,1)S(1)}, bf16[512,4,32]{2,0,1:T(8,128)(2,1)}, u32[]{:S(2)}) copy-start(bf16[512,4,32]{2,0,1:T(8,128)(2,1)} %get-tuple-element.11) | copy-start | bytes 393220
  539.5 5.9 %copy-start.1 = (s32[8,16]{1,0:T(8,128)S(1)}, s32[8,16]{1,0:T(8,128)}, u32[]{:S(2)}) copy-start(s32[8,16]{1,0:T(8,128)} %param.14) | copy-start | bytes 1540
Sparse Core Ops, SparseCore 0:
  10.0 83.3 all-gather.8
  96.0 79.0 all-gather.6
  177.7 116.9 all-gather.4
  390.3 92.7 all-gather.10
where the time goes:
time: 563 us; the launch traced here: 552 us
  waiting for transfers between devices  399 us (71%)
  matrix products  56.9 us (10%)
  blocking collectives  28.9 us (5%)
  local copies, waits for them, and re-layouts  28.1 us (5%)
  other arithmetic  19.7 us (3%)
  between operations  13.8 us (2%)
  starting transfers between devices  6.06 us (1%)
    ppermute x3, waiting for transfers between devices, shifted(): return lax.ppermute(block, axis, route)  153 us
    all_gather x1, waiting for transfers between devices, per_device(): lax.all_gather(qkv_broad, 'seq', axis=0, tiled=True)  107 us
    all_gather x1, waiting for transfers between devices, per_device(): downs = lax.all_gather(adapter_down, 'seq', axis=0, tiled=True)  75 us
    all_gather x1, waiting for transfers between devices, per_device(): ups = lax.all_gather(adapter_up, 'seq', axis=0, tiled=True)  63.4 us
    all_gather x1, blocking collectives, per_device(): lax.all_gather(qkv_weight, 'fsdp', axis=1, tiled=True)  14.7 us
    all_gather x1, blocking collectives, per_device(): lax.all_gather(out_weight, 'fsdp', axis=1, tiled=True)  14.2 us
    sub x1, matrix products, per_device(): weights = jnp.exp(scores - highest)  11.9 us
  transfers between devices with their start and end apart: 7, of which 6 were waited for; matrix products, arithmetic and copies ran while one was open for 13% of the time, Pallas kernels for 0%

commit v1 on v0

v1 whole, which is shorter than its diff:
```python
import functools

import jax
import jax.numpy as jnp
from jax import lax
from jax.experimental import pallas as pl
from jax.experimental.pallas import tpu as pltpu
from jax.sharding import PartitionSpec as P

HS = 256
SPAN = 3
MESH = pl.DeviceIdType.MESH

eps_norm = 1e-05
adapter_scale_factor = 0.5

NX, NY, NZ = 4, 4, 8


def gather_kernel(tokens, qkv, outw, down, up, wq, ws, halo, send, recv, local):
    f = lax.axis_index("fsdp")
    s = lax.axis_index("seq")
    x, c = f // 2, lax.rem(f, 2)
    y, z = s // NZ, lax.rem(s, NZ)

    def dev(dx=0, dy=0, dz=0, flip=0):
        xx = lax.rem(x + dx + NX, NX)
        yy = lax.rem(y + dy + NY, NY)
        zz = lax.rem(z + dz + NZ, NZ)
        cc = lax.rem(c + flip, 2)
        return {"fsdp": xx * 2 + cc, "seq": yy * NZ + zz}

    nxt = {"fsdp": f, "seq": lax.rem(s + 1, NY * NZ)}
    prv = {"fsdp": f, "seq": lax.rem(s + NY * NZ - 1, NY * NZ)}

    barrier = pltpu.get_barrier_semaphore()
    peers = [nxt, prv, dev(dz=1), dev(dz=-1), dev(dx=1), dev(dx=-1), dev(dy=1), dev(dy=-1), dev(flip=1)]
    for peer in peers:
        pl.semaphore_signal(barrier, inc=1, device_id=peer, device_id_type=MESH)
    pl.semaphore_wait(barrier, len(peers))

    names = {}

    def sem_of(name):
        return names.setdefault(name, len(names))

    sent = []

    def push(src, dst, name, peer):
        i = sem_of(name)
        copy = pltpu.make_async_remote_copy(
            src_ref=src, dst_ref=dst, send_sem=send.at[i], recv_sem=recv.at[i],
            device_id=peer, device_id_type=MESH,
        )
        copy.start()
        return copy

    def arrived(dst, name):
        i = sem_of(name)
        pltpu.make_async_remote_copy(
            src_ref=dst, dst_ref=dst, send_sem=send.at[i], recv_sem=recv.at[i],
            device_id=dev(), device_id_type=MESH,
        ).wait_recv()

    half = tokens.shape[0] // 2

    def rows(ref, k):
        return ref.at[pl.ds(k * half, half), :]

    for k in range(2):
        sent.append(push(rows(tokens, k), rows(halo.at[0], k), ("halo", 0, k), nxt))

    def hop(n):
        for k in range(2):
            arrived(rows(halo.at[n - 1], k), ("halo", n - 1, k))
            sent.append(push(rows(halo.at[n - 1], k), rows(halo.at[n], k), ("halo", n, k), nxt))

    def piece_q(zz):
        return wq.at[c, x, pl.ds(pl.multiple_of((y * NZ + zz) * 64, 64), 64), :]

    def piece_s(zz):
        return ws.at[c, x, :, pl.ds(pl.multiple_of((y * NZ + zz) * 32, 32), 32), :]

    cols = pl.ds(pl.multiple_of(f * 256, 256), 256)
    own = [
        pltpu.make_async_copy(qkv, piece_q(z), local.at[0]),
        pltpu.make_async_copy(outw, piece_s(z).at[0], local.at[1]),
        pltpu.make_async_copy(down.at[:, cols], piece_s(z).at[1], local.at[2]),
        pltpu.make_async_copy(up.at[:, cols], piece_s(z).at[2], local.at[3]),
    ]
    for copy in own:
        copy.start()
    for copy in own:
        copy.wait()

    for k in range(NZ - 1):
        zz = lax.rem(z + k, NZ)
        for name, piece in (("zq", piece_q), ("zs", piece_s)):
            if k > 0:
                arrived(piece(zz), (name, k - 1))
            sent.append(push(piece(zz), piece(zz), (name, k), dev(dz=-1)))
    zz = lax.rem(z + NZ - 1, NZ)
    arrived(piece_q(zz), ("zq", NZ - 2))
    arrived(piece_s(zz), ("zs", NZ - 2))

    def ring(pick, step, tag, on_ready):
        for a in range(2):
            for h, k in ((0, 1), (1, -1)):
                sent.append(push(pick(0, h, a), pick(0, h, a), (tag, "own", k, h, a), step(k)))
            for h, k in ((1, 1), (0, -1)):
                sent.append(push(pick(0, h, a), pick(0, h, a), (tag, "own", k, h, a), step(k)))
        yield
        for a in range(2):
            arrived(pick(-1, 0, a), (tag, "own", 1, 0, a))
            sent.append(push(pick(-1, 0, a), pick(-1, 0, a), (tag, "fwd", 1, a), step(1)))
            arrived(pick(1, 1, a), (tag, "own", -1, 1, a))
            sent.append(push(pick(1, 1, a), pick(1, 1, a), (tag, "fwd", -1, a), step(-1)))
            arrived(pick(-1, 1, a), (tag, "own", 1, 1, a))
            on_ready(-1, a)
            arrived(pick(1, 0, a), (tag, "own", -1, 0, a))
            on_ready(1, a)
        yield
        for a in range(2):
            arrived(pick(2, 0, a), (tag, "fwd", 1, a))
            arrived(pick(2, 1, a), (tag, "fwd", -1, a))
            on_ready(2, a)
        yield

    def nothing(d, a):
        pass

    def mid_y(d, h, a):
        yy = lax.rem(y + d + NY, NY)
        if a == 0:
            return wq.at[c, x, pl.ds(pl.multiple_of(yy * 512 + h * 256, 256), 256), :]
        return ws.at[c, x, :, pl.ds(pl.multiple_of(yy * 256 + h * 128, 128), 128), :]

    def mid_x(d, h, a):
        xx = lax.rem(x + d + NX, NX)
        if a == 0:
            return wq.at[c, xx, pl.ds(pl.multiple_of(y * 512 + h * 256, 256), 256), :]
        return ws.at[c, xx, :, pl.ds(pl.multiple_of(y * 256 + h * 128, 128), 128), :]

    def last_x(cc, d, h, a):
        xx = lax.rem(x + d + NX, NX)
        if a == 0:
            return wq.at[cc, xx, :, :] if h is None else wq.at[cc, xx, pl.ds(h * 1024, 1024), :]
        return ws.at[cc, xx, :, :, :] if h is None else ws.at[cc, xx, :, pl.ds(h * 512, 512), :]

    def last_y(cc, d, h, a):
        yy = lax.rem(y + d + NY, NY)
        if a == 0:
            base, size = (0, 512) if h is None else (h * 256, 256)
            return wq.at[cc, :, pl.ds(pl.multiple_of(yy * 512 + base, 256), size), :]
        base, size = (0, 256) if h is None else (h * 128, 128)
        return ws.at[cc, :, :, pl.ds(pl.multiple_of(yy * 256 + base, 128), size), :]

    def step_x(k):
        return dev(dx=k)

    def step_y(k):
        return dev(dy=k)

    def branch(mid, mid_step, last, last_step, other_last, cc):
        base = len(sent)
        for _ in ring(mid, mid_step, "mid", nothing):
            pass
        give = functools.partial(last, cc)

        def share(d, a):
            sent.append(push(give(d, None, a), give(d, None, a), ("core", d, a, cc), dev(flip=1)))

        steps = ring(give, last_step, "last", share)
        next(steps)
        share(0, 0)
        share(0, 1)
        hop(1)
        next(steps)
        hop(2)
        next(steps)
        for a in range(2):
            for d in (0, -1, 1, 2):
                arrived(other_last(1 - cc, d, None, a), ("core", d, a, 1 - cc))
        for k in range(2):
            arrived(rows(halo.at[2], k), ("halo", 2, k))
        for copy in sent[base:]:
            copy.wait_send()
        del sent[base:]

    @pl.when(c == 0)
    def _():
        branch(mid_y, step_y, last_x, step_x, last_y, 0)

    @pl.when(c == 1)
    def _():
        branch(mid_x, step_x, last_y, step_y, last_x, 1)

    for copy in sent:
        copy.wait_send()


def communicate(tokens, qkv_weight, out_weight, adapter_down, adapter_up):
    any_spec = pl.BlockSpec(memory_space=pl.ANY)
    bf16 = jnp.bfloat16
    return pl.pallas_call(
        gather_kernel,
        out_shape=(
            jax.ShapeDtypeStruct((2, NX, 2048, 384), bf16),
            jax.ShapeDtypeStruct((2, NX, 3, 1024, 256), bf16),
            jax.ShapeDtypeStruct((SPAN, 512, 2048), bf16),
        ),
        in_specs=[any_spec] * 5,
        out_specs=(any_spec,) * 3,
        scratch_shapes=[
            pltpu.SemaphoreType.DMA((100,)),
            pltpu.SemaphoreType.DMA((100,)),
            pltpu.SemaphoreType.DMA((4,)),
        ],
        compiler_params=pltpu.CompilerParams(collective_id=0, has_side_effects=True),
    )(tokens, qkv_weight, out_weight, adapter_down, adapter_up)


def layer_norm(token_rows):
    value_vectors = token_rows.astype(jnp.float32)
    average = jnp.mean(value_vectors, axis=-1, keepdims=True)
    centred = value_vectors - average
    variance = jnp.mean(centred * centred, axis=-1, keepdims=True)
    return (centred * lax.rsqrt(variance + eps_norm)).astype(jnp.bfloat16)


def request_info(length_row, position):
    row_ends = jnp.cumsum(length_row)
    request = jnp.sum((position[:, None] >= row_ends[None, :]).astype(jnp.int32), axis=1)
    onehot = (request[:, None] == jnp.arange(length_row.shape[0], dtype=jnp.int32)[None, :]).astype(
        jnp.int32
    )
    begins = jnp.sum(onehot * (row_ends - length_row)[None, :], axis=1)
    return (request, onehot, position - begins)


def rotate(head_rows, position):
    rotary = head_rows.shape[-1] // 4
    halfway = rotary // 2
    inverse = 10000.0 ** (-2.0 * jnp.arange(halfway, dtype=jnp.float32) / rotary)
    angles = position.astype(jnp.float32)[:, None] * inverse[None, :]
    cosine = jnp.cos(angles)[:, None, :]
    sine_part = jnp.sin(angles)[:, None, :]
    leading = head_rows[..., :halfway]
    trailing = head_rows[..., halfway:rotary]
    return jnp.concatenate(
        [
            leading * cosine - trailing * sine_part,
            trailing * cosine + leading * sine_part,
            head_rows[..., rotary:],
        ],
        axis=-1,
    )


def per_device(
    tokens, qkv_weight, out_weight, adapter_down, adapter_up, lengths, adapter_ids, adapter_slot
):
    count = tokens.shape[0]
    group_index = lax.axis_index("fsdp")
    block_index = lax.axis_index("seq")
    wq, ws, halo = communicate(
        tokens, qkv_weight, out_weight, adapter_down.reshape(32, 2048), adapter_up.reshape(32, 2048)
    )
    qkv_full = wq.transpose(2, 1, 0, 3).reshape(2048, 3072)
    small = ws.transpose(2, 3, 1, 0, 4).reshape(3, 1024, 2048)
    out_full = small[0]
    downs = small[1].reshape(64, 16, 2048)
    ups = small[2].reshape(64, 16, 2048)
    length_row = lax.dynamic_index_in_dim(lengths, group_index, 0, keepdims=False)
    ids_row = lax.dynamic_index_in_dim(adapter_ids, group_index, 0, keepdims=False)
    request_slot = adapter_slot[ids_row]
    picked_down = downs[request_slot]
    picked_up = ups[request_slot]
    window = jnp.concatenate([tokens[None], halo], axis=0).reshape(4 * count, 2048)
    depth = 4
    key_position = (
        (block_index - jnp.arange(depth, dtype=jnp.int32))[:, None] * count
        + jnp.arange(count, dtype=jnp.int32)[None, :]
    ).reshape(-1)
    key_request, key_onehot, key_offsets = request_info(length_row, key_position)
    position, request, offsets = key_position[:count], key_request[:count], key_offsets[:count]
    normed = layer_norm(window)
    ranks = jnp.einsum("td,ard->tar", normed, picked_down, preferred_element_type=jnp.float32)
    ranks = jnp.where(key_onehot[:, :, None] > 0, ranks, 0.0).astype(jnp.bfloat16)
    ranks = ranks.reshape(depth * count, 256)
    up_flat = picked_up.reshape(256, 2048)
    width = 1024
    query = jnp.dot(normed[:count], qkv_full[:, :width], preferred_element_type=jnp.float32)
    query = query + adapter_scale_factor * jnp.dot(
        ranks[:count], up_flat[:, :width], preferred_element_type=jnp.float32
    )
    keys = jnp.dot(normed, qkv_full[:, width : 2 * width], preferred_element_type=jnp.float32)
    values = jnp.dot(normed, qkv_full[:, 2 * width :], preferred_element_type=jnp.float32)
    values = values + adapter_scale_factor * jnp.dot(
        ranks, up_flat[:, width:], preferred_element_type=jnp.float32
    )
    query = rotate(query.reshape(count, 4, HS), offsets).astype(jnp.bfloat16)
    keys = rotate(keys.reshape(depth * count, 4, HS), key_offsets).astype(jnp.bfloat16)
    values = values.astype(jnp.bfloat16).reshape(depth * count, 4, HS)
    allowed = (
        (key_request[None, :] == request[:, None])
        & (key_position[None, :] >= 0)
        & (key_position[None, :] <= position[:, None])
    )
    scores = jnp.einsum("qhd,khd->hqk", query, keys, preferred_element_type=jnp.float32) * HS ** (-0.5)
    scores = jnp.where(allowed[None, :, :], scores, -1e30)
    highest = jnp.max(scores, axis=-1, keepdims=True)
    weights = jnp.exp(scores - highest)
    probs = (weights / jnp.sum(weights, axis=-1, keepdims=True)).astype(jnp.bfloat16)
    attended = jnp.einsum("hqk,khd->qhd", probs, values, preferred_element_type=jnp.float32)
    attended = attended.astype(jnp.bfloat16).reshape(count, width)
    mixed = jnp.dot(attended, out_full, preferred_element_type=jnp.float32)
    return mixed.astype(jnp.bfloat16)


def solution(mesh):
    in_specs = (
        P(("fsdp", "seq"), None),
        P("seq", "fsdp"),
        P("seq", "fsdp"),
        P("seq", None, None),
        P("seq", None, None),
        P(),
        P(),
        P(),
    )
    out_specs = P(("fsdp", "seq"), None)
    return jax.shard_map(
        per_device, mesh=mesh, in_specs=in_specs, out_specs=out_specs, check_vma=False
    )
```

time: 563 us -> 443 us (0.79)
  waiting for transfers between devices: 399 us -> 0 us
  Pallas kernels: 0 us -> 240 us
  local copies, waits for them, and re-layouts: 28.1 us -> 85.9 us
  other arithmetic: 19.7 us -> 50 us
  blocking collectives: 28.9 us -> 0 us
  between operations: 13.8 us -> 0.66 us
  starting transfers between devices: 6.06 us -> 0 us
    all_gather x4 -> x0, waiting for transfers between devices: 245 us -> none  [the longest x1 107 us: per_device(): lax.all_gather(qkv_broad, 'seq', axis=0, tiled=True)]
    pallas_call x0 -> x1, Pallas kernels: none -> 240 us  [communicate(): pl.pallas_call(gather_kernel, out_shape=(jax.ShapeDtypeStruct((2, NX, 204...]
    ppermute x3 -> x0, waiting for transfers between devices: 153 us -> none  [shifted(): return lax.ppermute(block, axis, route)]
    all_gather x2 -> x0, blocking collectives: 28.9 us -> none  [the longest x1 14.7 us: per_device(): lax.all_gather(qkv_weight, 'fsdp', axis=1, tiled=True)]
    slice x2 -> x8, local copies, waits for them, and re-layouts: 10.2 us -> 35.7 us  [the longest x2 15.5 us: per_device(): out_full = small[0]]
    sub x0 -> x1, other arithmetic: none -> 21.2 us  [per_device(): weights = jnp.exp(scores - highest)]
    transpose x0 -> x1, local copies, waits for them, and re-layouts: none -> 16.1 us  [per_device(): qkv_full = wq.transpose(2, 1, 0, 3).reshape(2048, 3072)]
    another operation x2, local copies, waits for them, and re-layouts: 0.82 us -> 16.4 us  [the longest x1 8.43 us: per_device(): ups = small[2].reshape(64, 16, 2048)]
  transfers between devices with their start and end apart: 7 -> 0, of which waited for: 6 -> 0; matrix products, arithmetic and copies ran while one was open for 13% -> 0% of each run, Pallas kernels for 0% -> 0%
where the time goes in v1:
time: 443 us; the launch traced here: 435 us
  Pallas kernels  240 us (54%)
  local copies, waits for them, and re-layouts  85.9 us (19%)
  matrix products  58.4 us (13%)
  other arithmetic  50 us (11%)
    pallas_call x1, Pallas kernels, communicate(): pl.pallas_call(gather_kernel, out_shape=(jax.ShapeDtypeStruct((2, NX, 204...  240 us
    sub x1, other arithmetic, per_device(): weights = jnp.exp(scores - highest)  21.2 us
    transpose x1, local copies, waits for them, and re-layouts, per_device(): qkv_full = wq.transpose(2, 1, 0, 3).reshape(2048, 3072)  16.1 us
    slice x2, local copies, waits for them, and re-layouts, per_device(): out_full = small[0]  15.5 us
    dot_general x1, matrix products, per_device(): jnp.dot(normed, qkv_full[:, width:2 * width], preferred_element_type=jnp....  13.6 us
    dot_general x1, matrix products, per_device(): jnp.dot(normed, qkv_full[:, 2 * width:], preferred_element_type=jnp.float32)  11.1 us
    convert_element_type x2, other arithmetic, layer_norm(): return (centred * lax.rsqrt(variance + eps_norm)).astype(jnp.bfloat16)  10.7 us
    dot_general x1, matrix products, per_device(): jnp.einsum('hqk,khd->qhd', probs, values, preferred_element_type=jnp.floa...  9.64 us

profile of v1, /device:TPU:8, one launch (start us, length us, event | category | flops | bytes accessed | tf_op | source)
XLA Modules:
  0.0 435.4 jit_solution(15164466741791478888)
XLA Ops:
  9.1 240.5 %shard_map.82 = (bf16[2,4,2048,384]{3,2,1,0:T(8,128)(2,1)}, bf16[2,4,3,1024,256]{4,3,2,1,0:T(8,128)(2,1)}, bf16[3,512,2048]{2,1,0:T(8,128)(2,1)}) custom-call(bf16[512,2048]{1,0:T(8,128)(2,1)} %tokens.1, bf16[64,384]{1,0:T(8,128)(2,1)} %qkv.1, bf16[32,256]{1,0:T(8,128)(2,1)} %outw.1, bf16[32,2048]{1,0:T(8,128)(2,1)} %bitcast.97, bf16[32,2048]{1,0:T(8,128)(2,1)} %bitcast.98), custom_call_target="tpu_custom_call" | custom-call | tf_op jit(solution)/shard_map/pallas_call | solution.py:205
  249.6 16.1 %copy.23 = bf16[2048,4,2,384]{0,3,2,1:T(8,128)(2,1)} copy(bf16[2048,4,2,384]{3,0,1,2:T(8,128)(2,1)} %bitcast.84) | data formatting | bytes 25165824 | tf_op jit(solution)/shard_map/transpose | solution.py:269
  265.8 9.0 %fusion.46 = (bf16[1,1024,4,2,256]{4,1,0,2,3:T(8,128)(2,1)}, bf16[1,1024,4,2,256]{4,1,0,2,3:T(8,128)(2,1)}, bf16[1,1024,4,2,256]{4,1,0,2,3:T(8,128)(2,1)}) fusion(bf16[3,1024,4,2,256]{4,1,0,2,3:T(8,128)(2,1)} %bitcast.83), kind=kLoop, calls=%fused_computation.84 | loop fusion | bytes 25165824 | tf_op jit(solution)/shard_map/slice | solution.py:271
  274.8 6.5 %copy.31 = bf16[1,1024,4,2,256]{1,4,3,2,0:T(8,128)(2,1)} copy(bf16[1,1024,4,2,256]{4,1,0,2,3:T(8,128)(2,1)} %get-tuple-element.13) | data formatting | bytes 8388608 | tf_op jit(solution)/shard_map/slice | solution.py:271
  281.2 4.7 %convert_reduce_fusion = f32[4,512]{1,0:T(4,128)S(1)} fusion(bf16[3,512,2048]{2,1,0:T(8,128)(2,1)} %get-tuple-element.8, bf16[1,512,2048]{2,1,0:T(8,128)(2,1)} %bitcast.74), kind=kLoop, calls=%fused_computation.12 | loop fusion | flops 12580864 | bytes 8396800 | tf_op jit(solution)/shard_map/reduce_sum | solution.py:225
  286.5 2.7 multiply_reduce_fusion
  289.2 8.4 %copy.26 = bf16[1,1024,4,2,256]{4,3,2,1,0:T(2,128)(2,1)} copy(bf16[1,1024,4,2,256]{4,1,0,2,3:T(8,128)(2,1)} %get-tuple-element.14) | data formatting | bytes 8388608 | tf_op jit(solution)/shard_map/slice | solution.py:273
  297.7 8.4 %reshape_squeeze.7 = bf16[64,16,2048]{2,1,0:T(8,128)(2,1)} reshape(bf16[1,1024,4,2,256]{4,3,2,1,0:T(2,128)(2,1)} %copy.26) | data formatting | bytes 8388608 | tf_op jit(solution)/shard_map/reshape;squeeze | solution.py:273
  306.1 2.8 gather_fusion.2
  308.9 8.4 %copy.25 = bf16[1,1024,4,2,256]{4,3,2,1,0:T(2,128)(2,1)} copy(bf16[1,1024,4,2,256]{4,1,0,2,3:T(8,128)(2,1)} %get-tuple-element.15) | data formatting | bytes 8388608 | tf_op jit(solution)/shard_map/slice | solution.py:272
  317.4 8.0 %reshape_squeeze.6 = bf16[64,16,2048]{2,1,0:T(8,128)(2,1)} reshape(bf16[1,1024,4,2,256]{4,3,2,1,0:T(2,128)(2,1)} %copy.25) | data formatting | bytes 8388608 | tf_op jit(solution)/shard_map/reshape;squeeze | solution.py:272
  325.4 3.8 gather_fusion.1
  329.1 2.5 slice.106
  331.7 6.1 %fusion.2 = bf16[2048,2048]{1,0:T(8,128)(2,1)S(1)} fusion(f32[2048]{0:T(1024)S(1)} %bitcast.100, f32[2048]{0:T(1024)S(1)} %bitcast.99, bf16[3,512,2048]{2,1,0:T(8,128)(2,1)} %get-tuple-element.8, bf16[1,512,2048]{2,1,0:T(8,128)(2,1)S(1)} %bitcast.76), kind=kLoop, calls=%fused_computation.6 | loop fusion | flops 20971520 | bytes 16793600 | tf_op jit(solution)/shard_map/convert_element_type | solution.py:228
  341.0 4.6 %multiply_convert_fusion = bf16[4,512,2048]{2,1,0:T(8,128)(2,1)} fusion(f32[4,512]{1,0:T(4,128)S(1)} %get-tuple-element.24, f32[4,512]{1,0:T(4,128)S(1)} %get-tuple-element.27, bf16[3,512,2048]{2,1,0:T(8,128)(2,1)S(1)} %bitcast.73, bf16[1,512,2048]{2,1,0:T(8,128)(2,1)S(1)} %bitcast.77), kind=kLoop, calls=%fused_computation.10 | loop fusion | flops 20971520 | bytes 16793600 | tf_op jit(solution)/shard_map/convert_element_type | solution.py:228
  345.6 13.6 %fusion.49 = f32[2048,4,256]{0,2,1:T(8,128)} fusion(bf16[2048,2048,1]{1,0,2:T(8,128)(2,1)} %bitcast.85, bf16[4,256,2048]{2,1,0:T(8,128)(2,1)S(1)} %bitcast.90), kind=kOutput, calls=%fused_computation.87 | convolution fusion | flops 8589934592 | bytes 20971520 | tf_op jit(solution)/shard_map/dot_general | solution.py:297
  359.3 2.8 subtract_convert_fusion
  362.1 5.0 %slice.127 = bf16[2048,4,192]{0,2,1:T(8,128)(2,1)} slice(f32[2048,4,256]{0,2,1:T(8,128)} %fusion.49), slice={[0:2048], [0:4], [64:256]} | slice | bytes 6291456 | tf_op jit(solution)/shard_map/slice | solution.py:254
  369.4 11.1 %fusion.12 = f32[2048,1024]{0,1:T(8,128)} fusion(bf16[2048,2048]{1,0:T(8,128)(2,1)S(1)} %fusion.2, bf16[2048,3072]{0,1:T(8,128)(2,1)S(1)} %bitcast.82), kind=kOutput, calls=%fused_computation.25 | convolution fusion | flops 8589934592 | bytes 20971520 | tf_op jit(solution)/shard_map/dot_general | solution.py:298
  380.5 6.7 %add_convert_fusion = bf16[2048,1024]{0,1:T(8,128)(2,1)} fusion(f32[2048,1024]{0,1:T(8,128)} %fusion.12, bf16[2048,256]{0,1:T(8,128)(2,1)S(1)} %bitcast.91, bf16[256,2048]{1,0:T(8,128)(2,1)S(1)} %bitcast.86), kind=kOutput, calls=%fused_computation.19 | convolution fusion | flops 1080033280 | bytes 14155776 | tf_op jit(solution)/shard_map/dot_general | solution.py:299
  393.5 7.1 %fusion.14 = f32[4,512,2048]{2,1,0:T(8,128)} fusion(bf16[2048,4,192]{0,2,1:T(8,128)(2,1)S(1)} %copy-done.4, bf16[2048,4,32]{0,2,1:T(8,128)(2,1)S(1)} %copy-done.7, bf16[2048,4,32]{0,2,1:T(8,128)(2,1)S(1)} %copy-done.6, bf16[512,4,192]{2,0,1:T(8,128)(2,1)S(1)} %copy.45, bf16[512,4,32]{2,0,1:T(8,128)(2,1)S(1)} %get-tuple-element.19, ...), kind=kOutput, calls=%fused_computation.27 | convolution fusion | flops 2163212288 | bytes 22020096 | tf_op jit(solution)/shard_map/qhd,khd->hqk/dot_general | solution.py:310
  400.6 21.2 %fusion.48 = (f32[4,512]{1,0:T(4,128)S(1)}, f32[4,512,2048]{2,1,0:T(8,128)}) fusion(f32[4,512,2048]{2,1,0:T(8,128)} %fusion.14, pred[512,2048]{1,0:T(8,128)(4,1)S(1)} %copy-done.15), kind=kOutput, calls=%fused_computation.86 | output fusion | flops 25167872 | bytes 34611200 | tf_op jit(solution)/shard_map/sub | solution.py:313
  421.8 9.6 %fusion.27 = bf16[4,256,512]{2,1,0:T(8,128)(2,1)S(1)} fusion(bf16[2048,4,256]{0,2,1:T(8,128)(2,1)} %bitcast.88, f32[4,512,2048]{2,1,0:T(8,128)} %get-tuple-element.33, f32[4,512]{1,0:T(4,128)S(1)} %get-tuple-element.32), kind=kOutput, calls=%fused_computation.40 | convolution fusion | flops 2156396544 | bytes 22028288 | tf_op jit(solution)/shard_map/hqk,khd->qhd/dot_general | solution.py:315
  431.5 3.7 convolution_convert_fusion
  (87 shorter events, 21.4 us)
Async XLA Ops:
  0.0 1.4 copy-start
  274.8 11.2 %slice-start = ((s8[6291456]{0:T(1024)(128)(4,1)}), s8[2097152]{0:T(1024)(128)(4,1)S(1)}, s32[]{:S(2)}) async-start(s8[6291456]{0:T(1024)(128)(4,1)} %bitcast.70), calls=%async_computation | async-start | bytes 4194304
  281.2 4.8 %copy-start.2 = (bf16[512,2048]{1,0:T(8,128)(2,1)S(1)}, bf16[512,2048]{1,0:T(8,128)(2,1)}, u32[]{:S(2)}) copy-start(bf16[512,2048]{1,0:T(8,128)(2,1)} %tokens.1) | copy-start | bytes 6291460
  281.2 5.2 %slice-start.1 = ((s8[6291456]{0:T(1024)(128)(4,1)}), s8[4194304]{0:T(1024)(128)(4,1)S(1)}, s32[]{:S(2)}) async-start(s8[6291456]{0:T(1024)(128)(4,1)} %bitcast.70), calls=%async_computation.1 | async-start | bytes 8388608
  317.4 14.3 %copy-start.3 = (bf16[512,2048]{1,0:T(8,128)(2,1)S(1)}, bf16[512,2048]{1,0:T(8,128)(2,1)}, u32[]{:S(2)}) copy-start(bf16[512,2048]{1,0:T(8,128)(2,1)} %tokens.1) | copy-start | bytes 6291460
  331.6 6.1 %copy-start.13 = (bf16[16,16,2048]{2,1,0:T(8,128)(2,1)S(1)}, bf16[16,16,2048]{2,1,0:T(8,128)(2,1)}, u32[]{:S(2)}) copy-start(bf16[16,16,2048]{2,1,0:T(8,128)(2,1)} %gather_fusion.1) | copy-start | bytes 3145732
  331.6 9.3 %slice-start.2 = ((s8[6291456]{0:T(1024)(128)(4,1)}), s8[4194304]{0:T(1024)(128)(4,1)S(1)}, s32[]{:S(2)}) async-start(s8[6291456]{0:T(1024)(128)(4,1)} %bitcast.72), calls=%async_computation.2 | async-start | bytes 8388608
  337.8 3.2 slice-start.3
  340.2 5.4 %copy-start.8 = (bf16[2048,16,16]{0,2,1:T(8,128)(2,1)}, bf16[2048,16,16]{0,2,1:T(8,128)(2,1)S(1)}, u32[]{:S(2)}) copy-start(bf16[2048,16,16]{0,2,1:T(8,128)(2,1)S(1)} %fusion.23) | copy-start | bytes 3145732
  341.0 26.0 %slice-start.4 = ((s8[12582912]{0:T(1024)(128)(4,1)}), s8[4194304]{0:T(1024)(128)(4,1)S(1)}, s32[]{:S(2)}) async-start(s8[12582912]{0:T(1024)(128)(4,1)} %bitcast.79), calls=%async_computation.4 | async-start | bytes 8388608
  345.6 13.7 %copy-start.11 = (f32[2048,32]{0,1:T(8,128)S(1)}, f32[2048,32]{0,1:T(8,128)}, u32[]{:S(2)}) copy-start(f32[2048,32]{0,1:T(8,128)} %get-tuple-element.22) | copy-start | bytes 786436
  345.6 13.7 %copy-start.12 = (f32[2048,32]{0,1:T(8,128)S(1)}, f32[2048,32]{0,1:T(8,128)}, u32[]{:S(2)}) copy-start(f32[2048,32]{0,1:T(8,128)} %get-tuple-element.23) | copy-start | bytes 786436
  345.6 21.4 %slice-start.5 = ((s8[12582912]{0:T(1024)(128)(4,1)}), s8[4194304]{0:T(1024)(128)(4,1)S(1)}, s32[]{:S(2)}) async-start(s8[12582912]{0:T(1024)(128)(4,1)} %bitcast.79), calls=%async_computation.5 | async-start | bytes 8388608
  345.6 21.4 %slice-start.6 = ((s8[12582912]{0:T(1024)(128)(4,1)}), s8[4194304]{0:T(1024)(128)(4,1)S(1)}, s32[]{:S(2)}) async-start(s8[12582912]{0:T(1024)(128)(4,1)} %bitcast.79), calls=%async_computation.6 | async-start | bytes 8388608
  369.4 11.1 %copy-start.9 = (bf16[2048,16,16]{0,2,1:T(8,128)(2,1)S(1)}, bf16[2048,16,16]{0,2,1:T(8,128)(2,1)}, u32[]{:S(2)}) copy-start(bf16[2048,16,16]{0,2,1:T(8,128)(2,1)} %copy-done.8) | copy-start | bytes 3145732
  380.5 6.7 %copy-start.14 = (bf16[512,16,16]{0,2,1:T(8,128)(2,1)S(1)}, bf16[512,16,16]{0,2,1:T(8,128)(2,1)}, u32[]{:S(2)}) copy-start(bf16[512,16,16]{0,2,1:T(8,128)(2,1)} %slice.100) | copy-start | bytes 786436
  389.1 4.3 copy-start.6
  389.1 4.3 copy-start.7
  391.6 1.5 copy-start.10
  391.6 2.0 copy-start.4
  393.5 7.1 %copy-start.15 = (pred[512,2048]{1,0:T(8,128)(4,1)S(1)}, pred[512,2048]{1,0:T(8,128)(4,1)}, u32[]{:S(2)}) copy-start(pred[512,2048]{1,0:T(8,128)(4,1)} %compare_and_fusion) | copy-start | bytes 3145732
  421.8 9.7 %copy-start.5 = (bf16[1,1024,4,2,256]{1,4,3,2,0:T(8,128)(2,1)S(1)}, bf16[1,1024,4,2,256]{1,4,3,2,0:T(8,128)(2,1)}, u32[]{:S(2)}) copy-start(bf16[1,1024,4,2,256]{1,4,3,2,0:T(8,128)(2,1)} %copy.31) | copy-start | bytes 12582916
  421.8 13.4 %copy-start.1 = (s32[64]{0:T(128)S(1)}, s32[64]{0:T(128)}, u32[]{:S(2)}) copy-start(s32[64]{0:T(128)} %param.15) | copy-start | bytes 772

commit v2 on v0

v2 whole, which is shorter than its diff:
```python
import functools

import jax
import jax.numpy as jnp
import numpy as np
from jax import lax
from jax.experimental import pallas as pl
from jax.experimental.pallas import tpu as pltpu
from jax.sharding import PartitionSpec as P

HS = 256
HEADS = 4
SPAN = 3
TOK = 512
REQS = 16
WIDTH = 1024
NX, NY, NZ = 4, 4, 8
MESH = pl.DeviceIdType.MESH
bf16, f32, i32 = jnp.bfloat16, jnp.float32, jnp.int32

eps_norm = 1e-05
adapter_scale_factor = 0.5


def whole_kernel(
    lengths, ids, slots, inverse, tokens, qkv, outw, down, up,
    out,
    wq, ws, H, stage, kbuf, vbuf, qbuf, onehot, dsel, usel, rbuf, acc, mbuf, lbuf, ctab, stab, begins, owner, bias, obuf,
    send, recv, local, osem,
):
    f = lax.axis_index("fsdp")
    s = lax.axis_index("seq")
    x, c = f // 2, lax.rem(f, 2)
    y, z = s // NZ, lax.rem(s, NZ)
    xs = {d: lax.rem(x + d + NX, NX) for d in (-1, 0, 1, 2)}
    ys = {d: lax.rem(y + d + NY, NY) for d in (-1, 0, 1, 2)}
    zs = {d: lax.rem(z + d, NZ) for d in range(NZ)}
    at = pl.multiple_of
    dev_x = {d: {"fsdp": xs[d] * 2 + c, "seq": s} for d in (1, -1)}
    dev_y = {d: {"fsdp": f, "seq": ys[d] * NZ + z} for d in (1, -1)}
    dev_z = {d: {"fsdp": f, "seq": y * NZ + zs[d % NZ]} for d in (1, -1)}
    dev_c = {"fsdp": x * 2 + (1 - c), "seq": s}
    self_id = {"fsdp": f, "seq": s}

    q_piece = {d: at((y * NZ + zs[d]) * 64, 64) for d in range(NZ)}
    s_piece = {d: at((y * NZ + zs[d]) * 32, 32) for d in range(NZ)}
    q_rows = {d: {h: at(ys[d] * 512 + o, 256) for h, o in ((None, 0), (0, 0), (1, 256))} for d in ys}
    s_rows = {d: {h: at(ys[d] * 256 + o, 128) for h, o in ((None, 0), (0, 0), (1, 128))} for d in ys}
    cols = pl.ds(at(f * 256, 256), 256)

    load = pltpu.make_async_copy(tokens, H.at[0], local.at[4])
    load.start()

    def piece_q(d):
        return wq.at[c, x, :, pl.ds(q_piece[d], 64), :]

    def piece_s(d):
        return ws.at[c, x, :, pl.ds(s_piece[d], 32), :]

    own = [
        pltpu.make_async_copy(outw, piece_s(0).at[0], local.at[0]),
        pltpu.make_async_copy(down.at[:, cols], piece_s(0).at[1], local.at[1]),
        pltpu.make_async_copy(up.at[:, cols], piece_s(0).at[2], local.at[2]),
    ] + [
        pltpu.make_async_copy(qkv.at[:, pl.ds(t * 128, 128)], piece_q(0).at[t], local.at[5 + t])
        for t in range(3)
    ]
    for copy in own:
        copy.start()

    barrier = pltpu.get_barrier_semaphore()
    peers = [dev_x[1], dev_x[-1], dev_y[1], dev_y[-1], dev_z[1], dev_z[-1], dev_c]
    for peer in peers:
        pl.semaphore_signal(barrier, inc=1, device_id=peer, device_id_type=MESH)
    pl.semaphore_wait(barrier, len(peers))

    names = {}

    def sem_of(name):
        return names.setdefault(name, len(names))

    def push(src, dst, name, peer, recv_name=None):
        copy = pltpu.make_async_remote_copy(
            src_ref=src, dst_ref=dst,
            send_sem=send.at[sem_of(name)], recv_sem=recv.at[sem_of(recv_name or name)],
            device_id=peer, device_id_type=MESH,
        )
        copy.start()
        return copy

    def arrived(dst, name):
        i = sem_of(name)
        pltpu.make_async_remote_copy(
            src_ref=dst, dst_ref=dst, send_sem=send.at[i], recv_sem=recv.at[i],
            device_id=self_id, device_id_type=MESH,
        ).wait_recv()

    def departed(src, name):
        i = sem_of(name)
        pltpu.make_async_remote_copy(
            src_ref=src, dst_ref=src, send_sem=send.at[i], recv_sem=recv.at[i],
            device_id=self_id, device_id_type=MESH,
        ).wait_send()

    half = TOK // 2

    def part(n, k):
        return H.at[n, pl.ds(k * half, half), :]

    def hop_part(n, k):
        @pl.when(z != NZ - 1)
        def _():
            push(part(n, k), part(n + 1, k), ("halo", n, k), dev_z[1])

        @pl.when(z == NZ - 1)
        def _():
            push(part(n, k), stage.at[n], ("halo", n, k), dev_z[1] if k == 0 else dev_y[1], ("stage", n))

    def hop(n):
        for k in range(2):
            arrived(part(n, k), ("halo", n - 1, k))
            hop_part(n, k)

    def relay(n):
        @pl.when(z == 0)
        def _():
            arrived(stage.at[n], ("stage", n))
            push(stage.at[n], part(n + 1, 0), ("relay", n), dev_y[1], ("halo", n, 0))

        @pl.when(z == NZ - 1)
        def _():
            arrived(stage.at[n], ("stage", n))
            push(stage.at[n], part(n + 1, 1), ("relay", n), dev_z[1], ("halo", n, 1))

    load.wait()
    for k in range(2):
        @pl.loop(0, half // 32)
        def _(i):
            r = pl.ds(at(k * half + i * 32, 32), 32)
            v = H[0, r, :].astype(f32)
            mean = jnp.mean(v, axis=-1, keepdims=True)
            centred = v - mean
            variance = jnp.mean(centred * centred, axis=-1, keepdims=True)
            H[0, r, :] = (centred * lax.rsqrt(variance + eps_norm)).astype(bf16)

        hop_part(0, k)

    for copy in own:
        copy.wait()

    for k in range(NZ - 1):
        for name, piece in (("zq", piece_q), ("zs", piece_s)):
            if k > 0:
                arrived(piece(k), (name, k - 1))
            push(piece(k), piece(k), (name, k), dev_z[-1])

    def end_z(name, piece):
        arrived(piece(NZ - 1), (name, NZ - 2))

    def rows_of(table, base, size):
        return pl.ds(base, size)

    def mid_y(d, h, a):
        if a == 0:
            return wq.at[c, x, :, pl.ds(q_rows[d][h], 256), :]
        return ws.at[c, x, :, pl.ds(s_rows[d][h], 128), :]

    def mid_x(d, h, a):
        if a == 0:
            return wq.at[c, xs[d], :, pl.ds(q_rows[0][h], 256), :]
        return ws.at[c, xs[d], :, pl.ds(s_rows[0][h], 128), :]

    def last_x(cc, d, h, a):
        if a == 0:
            return wq.at[cc, xs[d]] if h is None else wq.at[cc, xs[d], :, pl.ds(h * 1024, 1024), :]
        return ws.at[cc, xs[d]] if h is None else ws.at[cc, xs[d], :, pl.ds(h * 512, 512), :]

    def last_y(cc, d, h, a):
        if a == 0:
            return wq.at[cc, :, :, pl.ds(q_rows[d][h], 512 if h is None else 256), :]
        return ws.at[cc, :, :, pl.ds(s_rows[d][h], 256 if h is None else 128), :]

    class Ring:
        def __init__(self, pick, devs, tag):
            self.pick, self.devs, self.tag = pick, devs, tag

        def begin(self, a):
            for h, k in ((0, 1), (1, -1), (1, 1), (0, -1)):
                push(self.pick(0, h, a), self.pick(0, h, a), (self.tag, "own", k, h, a), self.devs[k])

        def forward(self, a):
            for k, h in ((1, 0), (-1, 1)):
                arrived(self.pick(-k, h, a), (self.tag, "own", k, h, a))
                push(self.pick(-k, h, a), self.pick(-k, h, a), (self.tag, "fwd", k, a), self.devs[k])

        def near(self, a):
            for k, h in ((1, 1), (-1, 0)):
                arrived(self.pick(-k, h, a), (self.tag, "own", k, h, a))

        def far(self, a):
            for k, h in ((1, 0), (-1, 1)):
                arrived(self.pick(2, h, a), (self.tag, "fwd", k, a))

        def drain(self):
            for a in range(2):
                for h, k in ((0, 1), (1, -1), (1, 1), (0, -1)):
                    departed(self.pick(0, h, a), (self.tag, "own", k, h, a))
                for k, h in ((1, 0), (-1, 1)):
                    departed(self.pick(-k, h, a), (self.tag, "fwd", k, a))

    plans = []
    for cc, mid, mid_devs, last, last_devs, other in (
        (0, mid_y, dev_y, last_x, dev_x, last_y),
        (1, mid_x, dev_x, last_y, dev_y, last_x),
    ):
        plans.append((
            Ring(mid, mid_devs, "mid"),
            Ring(functools.partial(last, cc), last_devs, "last"),
            functools.partial(last, cc),
            functools.partial(other, 1 - cc),
            cc,
        ))

    def per_core(body):
        for plan in plans:
            @pl.when(c == plan[4])
            def _():
                body(*plan)

    def share(give, cc, a, *ds):
        for d in ds:
            push(give(d, None, a), give(d, None, a), ("core", d, a, cc), dev_c)

    def first(mid, last, give, take, cc):
        end_z("zq", piece_q)
        mid.begin(0)
        end_z("zs", piece_s)
        mid.forward(0)
        mid.begin(1)
        mid.near(0)
        mid.far(0)
        last.begin(0)
        share(give, cc, 0, 0)
        mid.forward(1)
        mid.near(1)
        mid.far(1)

    def second(mid, last, give, take, cc):
        last.forward(0)
        last.begin(1)
        share(give, cc, 1, 0)
        last.near(0)
        share(give, cc, 0, -1, 1)

    def third(mid, last, give, take, cc):
        last.far(0)
        share(give, cc, 0, 2)
        last.forward(1)
        last.near(1)
        share(give, cc, 1, -1, 1)

    def fourth(mid, last, give, take, cc):
        last.far(1)
        share(give, cc, 1, 2)

    def fifth(mid, last, give, take, cc):
        for a in range(2):
            for d in (0, -1, 1, 2):
                arrived(take(d, None, a), ("core", d, a, 1 - cc))

    def drain(mid, last, give, take, cc):
        mid.drain()
        last.drain()
        for a in range(2):
            for d in (0, -1, 1, 2):
                departed(give(d, None, a), ("core", d, a, cc))

    per_core(first)
    relay(0)

    lane = lax.broadcasted_iota(i32, (TOK, 128), 1)
    token = lax.broadcasted_iota(i32, (TOK, 128), 0)

    @pl.loop(0, SPAN + 1)
    def _(j):
        position = (s - j) * TOK + token
        ends = jnp.int32(0)
        begin = jnp.zeros((TOK, 128), i32)
        request = jnp.zeros((TOK, 128), i32)
        for r in range(REQS - 1):
            ends = ends + lengths[f, r]
            past = position >= ends
            begin = jnp.where(past, ends, begin)
            request = request + past.astype(i32)
        begins[j] = begin
        owner[j] = request
        angle = (position - begin).astype(f32) * inverse[0:1, :]
        ctab[j] = jnp.where(lane < 64, jnp.cos(angle), 1.0)
        sine = jnp.sin(angle)
        stab[j] = jnp.where(lane < 32, -sine, jnp.where(lane < 64, sine, 0.0))

    per_core(second)
    hop(1)
    per_core(third)
    relay(1)
    per_core(fourth)
    hop(2)
    per_core(fifth)

    table = slots[...].astype(f32)
    at_slot = lax.broadcasted_iota(i32, (1, 64), 1)
    inner = lax.broadcasted_iota(i32, (16, 1024), 0)
    column = lax.broadcasted_iota(i32, (16, 1024), 1)
    for r in range(REQS):
        slot = jnp.sum(jnp.where(at_slot == ids[f, r], table, 0.0), axis=-1, keepdims=True)
        hit = column == slot.astype(i32) * 16 + inner
        onehot[r * 16 : (r + 1) * 16, :] = jnp.where(hit, 1.0, 0.0).astype(bf16)

    for g in range(8):
        for n, picked in ((1, dsel), (2, usel)):
            picked[:, g * 256 : (g + 1) * 256] = jnp.dot(
                onehot[...], ws[g % 2, g // 2, n], preferred_element_type=f32
            ).astype(bf16)

    def weight(tile):
        g = tile // 3
        return wq[lax.rem(g, 2), g // 2, lax.rem(tile, 3)]

    def columns(head):
        return jnp.concatenate([weight(2 * head), weight(2 * head + 1)], axis=1)

    def dot(a, b):
        return jnp.dot(a, b, preferred_element_type=f32)

    def rotated(v, j):
        first_half = v[:, :128]
        swapped = jnp.where(
            lane < 32, pltpu.roll(first_half, 96, 1), pltpu.roll(first_half, 32, 1)
        )
        return jnp.concatenate([first_half * ctab[j] + swapped * stab[j], v[:, 128:]], axis=1)

    def ranks(j):
        r = lax.dot_general(H[j], dsel[...], (((1,), (1,)), ((), ())), preferred_element_type=f32)
        column = lax.broadcasted_iota(i32, (TOK, 256), 1) // 16
        request = jnp.concatenate([owner[j]] * 2, axis=1)
        rbuf[...] = jnp.where(column == request, r, 0.0).astype(bf16)

    def scatter_bias(j):
        begin = jnp.concatenate([begins[0]] * 4, axis=1)
        row = lax.broadcasted_iota(i32, (TOK, TOK), 0) + s * TOK
        col = lax.broadcasted_iota(i32, (TOK, TOK), 1) + (s - j) * TOK
        bias[...] = jnp.where((col >= begin) & (col <= row), 0.0, -1e30).astype(f32)

    def block(j):
        ranks(j)
        scatter_bias(j)

        @pl.loop(0, HEADS)
        def _(h):
            u = usel[:, pl.ds(at(h * HS + WIDTH, HS), HS)]
            kbuf[...] = rotated(dot(H[j], columns(HEADS + h)), j).astype(bf16)
            value = dot(H[j], columns(2 * HEADS + h)) + adapter_scale_factor * dot(rbuf[...], u)
            vbuf[...] = value.astype(bf16)
            if j == 0:
                uq = usel[:, pl.ds(at(h * HS, HS), HS)]
                q = dot(H[0], columns(h)) + adapter_scale_factor * dot(rbuf[...], uq)
                qbuf[h] = rotated(q, 0).astype(bf16) * jnp.asarray(HS ** (-0.5), bf16)

            @pl.loop(0, 2)
            def _(i):
                r = pl.ds(at(i * 256, 256), 256)
                scores = lax.dot_general(
                    qbuf[h, r, :], kbuf[...], (((1,), (1,)), ((), ())), preferred_element_type=f32
                ) + bias[r, :]
                top = jnp.max(scores, axis=-1, keepdims=True)
                if j == 0:
                    p = jnp.exp(scores - top)
                    total = jnp.sum(p, axis=-1, keepdims=True)
                    acc[h, r, :] = dot(p.astype(bf16), vbuf[...])
                else:
                    before = mbuf[h, r, :][:, :1]
                    top = jnp.maximum(top, before)
                    fade = jnp.exp(before - top)
                    p = jnp.exp(scores - top)
                    total = fade * lbuf[h, r, :][:, :1] + jnp.sum(p, axis=-1, keepdims=True)
                    acc[h, r, :] = fade * acc[h, r, :] + dot(p.astype(bf16), vbuf[...])
                if j == SPAN:
                    qbuf[h, r, :] = (acc[h, r, :] / total).astype(bf16)
                else:
                    mbuf[h, r, :] = jnp.broadcast_to(top, (256, 128))
                    lbuf[h, r, :] = jnp.broadcast_to(total, (256, 128))

    block(0)
    block(1)
    relay(2)
    block(2)
    for k in range(2):
        arrived(part(3, k), ("halo", 2, k))
    block(3)

    for g in range(8):
        if g >= 2:
            pltpu.make_async_copy(obuf.at[g % 2], out.at[:, pl.ds((g - 2) * 256, 256)], osem.at[g % 2]).wait()
        attended = jnp.concatenate([qbuf[h] for h in range(HEADS)], axis=1)
        obuf[g % 2] = dot(attended, ws[g % 2, g // 2, 0]).astype(bf16)
        pltpu.make_async_copy(obuf.at[g % 2], out.at[:, pl.ds(g * 256, 256)], osem.at[g % 2]).start()
    for g in (6, 7):
        pltpu.make_async_copy(obuf.at[g % 2], out.at[:, pl.ds(g * 256, 256)], osem.at[g % 2]).wait()

    for n in range(SPAN):
        for k in range(2):
            departed(part(n, k), ("halo", n, k))

        @pl.when((z == 0) | (z == NZ - 1))
        def _():
            departed(stage.at[n], ("relay", n))
    for k in range(NZ - 1):
        departed(piece_q(k), ("zq", k))
        departed(piece_s(k), ("zs", k))
    per_core(drain)


def run_whole(lengths, ids, slots, inverse, tokens, qkv_weight, out_weight, down, up):
    anywhere = pl.BlockSpec(memory_space=pl.ANY)
    scalar = pl.BlockSpec(memory_space=pltpu.SMEM)
    return pl.pallas_call(
        whole_kernel,
        out_shape=jax.ShapeDtypeStruct((TOK, 2 * WIDTH), bf16),
        in_specs=[scalar] * 2 + [pl.BlockSpec(memory_space=pltpu.VMEM)] * 2 + [anywhere] * 5,
        out_specs=anywhere,
        scratch_shapes=[
            pltpu.VMEM((2, NX, 3, 2048, 128), bf16),
            pltpu.VMEM((2, NX, 3, 1024, 256), bf16),
            pltpu.VMEM((SPAN + 1, TOK, 2048), bf16),
            pltpu.VMEM((SPAN, TOK // 2, 2048), bf16),
            pltpu.VMEM((TOK, HS), bf16),
            pltpu.VMEM((TOK, HS), bf16),
            pltpu.VMEM((HEADS, TOK, HS), bf16),
            pltpu.VMEM((256, 1024), bf16),
            pltpu.VMEM((256, 2048), bf16),
            pltpu.VMEM((256, 2048), bf16),
            pltpu.VMEM((TOK, 256), bf16),
            pltpu.VMEM((HEADS, TOK, HS), f32),
            pltpu.VMEM((HEADS, TOK, 128), f32),
            pltpu.VMEM((HEADS, TOK, 128), f32),
            pltpu.VMEM((SPAN + 1, TOK, 128), f32),
            pltpu.VMEM((SPAN + 1, TOK, 128), f32),
            pltpu.VMEM((SPAN + 1, TOK, 128), i32),
            pltpu.VMEM((SPAN + 1, TOK, 128), i32),
            pltpu.VMEM((TOK, TOK), f32),
            pltpu.VMEM((2, TOK, 256), bf16),
            pltpu.SemaphoreType.DMA((110,)),
            pltpu.SemaphoreType.DMA((110,)),
            pltpu.SemaphoreType.DMA((8,)),
            pltpu.SemaphoreType.DMA((2,)),
        ],
        compiler_params=pltpu.CompilerParams(
            collective_id=0, has_side_effects=True, vmem_limit_bytes=62 * 1024 * 1024
        ),
    )(lengths, ids, slots, inverse, tokens, qkv_weight, out_weight, down, up)


def per_device(
    tokens, qkv_weight, out_weight, adapter_down, adapter_up, lengths, adapter_ids, adapter_slot
):
    rotary = HS // 4
    inverse = 10000.0 ** (-2.0 * (np.arange(128) % (rotary // 2)) / rotary)
    inverse = jnp.asarray(np.tile(inverse[None, :], (8, 1)), f32)
    return run_whole(
        lengths, adapter_ids, adapter_slot.reshape(1, -1), inverse, tokens, qkv_weight, out_weight,
        adapter_down.reshape(-1, 2048), adapter_up.reshape(-1, 2048),
    )


def solution(mesh):
    in_specs = (
        P(("fsdp", "seq"), None),
        P("seq", "fsdp"),
        P("seq", "fsdp"),
        P("seq", None, None),
        P("seq", None, None),
        P(),
        P(),
        P(),
    )
    out_specs = P(("fsdp", "seq"), None)
    return jax.shard_map(
        per_device, mesh=mesh, in_specs=in_specs, out_specs=out_specs, check_vma=False
    )
```

time: 563 us -> 217 us (0.39)
  the two profiles are of different devices: /device:TPU:8 before, /device:TPU:1 now
where the time goes in v2:
time: 217 us
  Pallas kernels  214 us (99%)
  local copies, waits for them, and re-layouts  3.16 us (1%)
    pallas_call x1, Pallas kernels, run_whole(): pl.pallas_call(whole_kernel, out_shape=jax.ShapeDtypeStruct((TOK, 2 * WID...  214 us

profile of v2, /device:TPU:1, one launch (start us, length us, event | category | flops | bytes accessed | tf_op | source)
XLA Modules:
  0.0 217.1 jit_solution(8452692232143939542)
XLA Ops:
  0.0 213.9 %shard_map.91 = bf16[512,2048]{1,0:T(8,128)(2,1)} custom-call(s32[8,16]{1,0:T(8,128)} %lengths.1, s32[8,16]{1,0:T(8,128)} %ids.1, s32[1,64]{1,0:T(1,128)} %bitcast.5, f32[8,128]{1,0:T(8,128)} %constant.2.clone.inverse, bf16[512,2048]{1,0:T(8,128)(2,1)} %tokens.1, bf16[64,384]{1,0:T(8,128)(2,1)} %qkv.1, bf16[32,256]{1,0:T(8,128)(2,1)} %outw.1, ...), custom_call_target="tpu_custom_call" | custom-call | tf_op jit(solution)/shard_map/pallas_call | solution.py:426
  214.0 3.2 %copy.11 = bf16[512,2048]{1,0:T(8,128)(2,1)} copy(bf16[512,2048]{1,0:T(8,128)(2,1)} %shard_map.91) | data formatting | bytes 4194304

commit v3 on v2

v3 whole, which is shorter than its diff:
```python
import functools

import jax
import jax.numpy as jnp
import numpy as np
from jax import lax
from jax.experimental import pallas as pl
from jax.experimental.pallas import tpu as pltpu
from jax.sharding import PartitionSpec as P

HS = 256
HEADS = 4
SPAN = 3
TOK = 512
REQS = 16
WIDTH = 1024
NX, NY, NZ = 4, 4, 8
MESH = pl.DeviceIdType.MESH
HEADS_AT_ONCE = 1
DETOUR = True
bf16, f32, i32 = jnp.bfloat16, jnp.float32, jnp.int32

eps_norm = 1e-05
adapter_scale_factor = 0.5


def whole_kernel(
    lengths, ids, slots, inverse, tokens, qkv, outw, down, up,
    out,
    wq, ws, H, kbuf, vbuf, qbuf, onehot, dsel, usel, rbuf, acc, vpre, mbuf, lbuf, ctab, stab, begins, owner, bias, obuf, att,
    send, recv, local, osem,
):
    f = lax.axis_index("fsdp")
    s = lax.axis_index("seq")
    x, c = f // 2, lax.rem(f, 2)
    y, z = s // NZ, lax.rem(s, NZ)
    xs = {d: lax.rem(x + d + NX, NX) for d in (-1, 0, 1, 2)}
    ys = {d: lax.rem(y + d + NY, NY) for d in (-1, 0, 1, 2)}
    zs = {d: lax.rem(z + d, NZ) for d in range(NZ)}
    at = pl.multiple_of
    dev_x = {d: {"fsdp": xs[d] * 2 + c, "seq": s} for d in (1, -1)}
    dev_y = {d: {"fsdp": f, "seq": ys[d] * NZ + z} for d in (1, -1)}
    dev_z = {d: {"fsdp": f, "seq": y * NZ + zs[d % NZ]} for d in (1, -1)}
    dev_c = {"fsdp": x * 2 + (1 - c), "seq": s}
    self_id = {"fsdp": f, "seq": s}

    q_piece = {d: at((y * NZ + zs[d]) * 64, 64) for d in range(NZ)}
    s_piece = {d: at((y * NZ + zs[d]) * 32, 32) for d in range(NZ)}
    q_rows = {d: {h: at(ys[d] * 512 + o, 256) for h, o in ((None, 0), (0, 0), (1, 256))} for d in ys}
    s_rows = {d: {h: at(ys[d] * 256 + o, 128) for h, o in ((None, 0), (0, 0), (1, 128))} for d in ys}
    cols = pl.ds(at(f * 256, 256), 256)

    load = pltpu.make_async_copy(tokens, H.at[0], local.at[4])
    load.start()

    def piece_q(d):
        return wq.at[c, x, :, pl.ds(q_piece[d], 64), :]

    def piece_s(d):
        return ws.at[c, x, :, pl.ds(s_piece[d], 32), :]

    own = [
        pltpu.make_async_copy(outw, piece_s(0).at[0], local.at[0]),
        pltpu.make_async_copy(down.at[:, cols], piece_s(0).at[1], local.at[1]),
        pltpu.make_async_copy(up.at[:, cols], piece_s(0).at[2], local.at[2]),
    ] + [
        pltpu.make_async_copy(qkv.at[:, pl.ds(t * 128, 128)], piece_q(0).at[t], local.at[5 + t])
        for t in range(3)
    ]
    for copy in own:
        copy.start()

    barrier = pltpu.get_barrier_semaphore()
    total = NY * NZ
    following = {"fsdp": f, "seq": lax.rem(s + 1, total)}
    preceding = {"fsdp": f, "seq": lax.rem(s + total - 1, total)}
    peers = [following, preceding, dev_x[1], dev_x[-1], dev_y[1], dev_y[-1], dev_z[1], dev_z[-1], dev_c]
    for peer in peers:
        pl.semaphore_signal(barrier, inc=1, device_id=peer, device_id_type=MESH)
    pl.semaphore_wait(barrier, len(peers))

    names = {}

    def sem_of(name):
        return names.setdefault(name, len(names))

    def push(src, dst, name, peer, recv_name=None):
        copy = pltpu.make_async_remote_copy(
            src_ref=src, dst_ref=dst,
            send_sem=send.at[sem_of(name)], recv_sem=recv.at[sem_of(recv_name or name)],
            device_id=peer, device_id_type=MESH,
        )
        copy.start()
        return copy

    def arrived(dst, name):
        i = sem_of(name)
        pltpu.make_async_remote_copy(
            src_ref=dst, dst_ref=dst, send_sem=send.at[i], recv_sem=recv.at[i],
            device_id=self_id, device_id_type=MESH,
        ).wait_recv()

    def departed(src, name):
        i = sem_of(name)
        pltpu.make_async_remote_copy(
            src_ref=src, dst_ref=src, send_sem=send.at[i], recv_sem=recv.at[i],
            device_id=self_id, device_id_type=MESH,
        ).wait_send()

    half = TOK // 2

    def part(n, k):
        return H.at[n, pl.ds(k * half, half), :]

    def hop_part(n, k):
        push(part(n, k), part(n + 1, k), ("halo", n, k), following)

    def hop(n):
        for k in range(2):
            arrived(part(n, k), ("halo", n - 1, k))
            hop_part(n, k)

    lane = lax.broadcasted_iota(i32, (TOK, 128), 1)
    token = lax.broadcasted_iota(i32, (TOK, 128), 0)

    def norm(k):
        @pl.loop(0, half // 64)
        def _(i):
            r = pl.ds(at(k * half + i * 64, 64), 64)
            v = H[0, r, :].astype(f32)
            mean = jnp.mean(v, axis=-1, keepdims=True)
            centred = v - mean
            variance = jnp.mean(centred * centred, axis=-1, keepdims=True)
            H[0, r, :] = (centred * lax.rsqrt(variance + eps_norm)).astype(bf16)

    def tables(j):
        position = (s - j) * TOK + token
        ends = jnp.int32(0)
        begin = jnp.zeros((TOK, 128), i32)
        request = jnp.zeros((TOK, 128), i32)
        for r in range(REQS - 1):
            ends = ends + lengths[f, r]
            past = position >= ends
            begin = jnp.where(past, ends, begin)
            request = request + past.astype(i32)
        if j == 0:
            begins[...] = begin
        owner[j] = request
        angle = (position - begin).astype(f32) * inverse[0:1, :]
        ctab[j] = jnp.where(lane < 64, jnp.cos(angle), 1.0)
        sine = jnp.sin(angle)
        stab[j] = jnp.where(lane < 32, -sine, jnp.where(lane < 64, sine, 0.0))

    def z_step(k):
        for name, piece in (("zq", piece_q), ("zs", piece_s)):
            if k > 0:
                arrived(piece(k), (name, k - 1))
            push(piece(k), piece(k), (name, k), dev_z[-1])

    load.wait()
    norm(0)
    hop_part(0, 0)
    for copy in own:
        copy.wait()
    z_step(0)
    norm(1)
    hop_part(0, 1)
    z_step(1)
    for k in range(2, NZ - 1):
        z_step(k)
        if k - 2 <= SPAN:
            tables(k - 2)

    def end_z(name, piece):
        arrived(piece(NZ - 1), (name, NZ - 2))

    def mid_y(d, h, a):
        if a == 0:
            return wq.at[c, x, :, pl.ds(q_rows[d][h], 256), :]
        return ws.at[c, x, :, pl.ds(s_rows[d][h], 128), :]

    def mid_x(d, h, a):
        if a == 0:
            return wq.at[c, xs[d], :, pl.ds(q_rows[0][h], 256), :]
        return ws.at[c, xs[d], :, pl.ds(s_rows[0][h], 128), :]

    def last_x(cc, d, h, a):
        if a == 0:
            return wq.at[cc, xs[d]] if h is None else wq.at[cc, xs[d], :, pl.ds(h * 1024, 1024), :]
        return ws.at[cc, xs[d]] if h is None else ws.at[cc, xs[d], :, pl.ds(h * 512, 512), :]

    def last_y(cc, d, h, a):
        if a == 0:
            return wq.at[cc, :, :, pl.ds(q_rows[d][h], 512 if h is None else 256), :]
        return ws.at[cc, :, :, pl.ds(s_rows[d][h], 256 if h is None else 128), :]

    inner_plane = z != 0

    class Ring:
        def __init__(self, pick, devs, tag, detour=False):
            self.pick, self.devs, self.tag, self.detour = pick, devs, tag, detour

        def send(self, d, h, a, name, k):
            if self.detour and k == 1:
                @pl.when(inner_plane)
                def _():
                    push(self.pick(d, h, a), self.pick(d, h, a), name, self.devs[k])
            else:
                push(self.pick(d, h, a), self.pick(d, h, a), name, self.devs[k])

        def get(self, d, h, a, name, k):
            arrived(self.pick(d, h, a), name)
            if self.detour and k == 1:
                @pl.when(z == 1)
                def _():
                    push(self.pick(d, h, a), self.pick(d, h, a), ("detour",) + name, dev_z[-1], name)

        def begin(self, a):
            for h, k in ((0, 1), (1, -1), (1, 1), (0, -1)):
                self.send(0, h, a, (self.tag, "own", k, h, a), k)

        def forward(self, a):
            for k, h in ((1, 0), (-1, 1)):
                self.get(-k, h, a, (self.tag, "own", k, h, a), k)
                self.send(-k, h, a, (self.tag, "fwd", k, a), k)

        def near(self, a):
            for k, h in ((1, 1), (-1, 0)):
                self.get(-k, h, a, (self.tag, "own", k, h, a), k)

        def far(self, a):
            for k, h in ((1, 0), (-1, 1)):
                self.get(2, h, a, (self.tag, "fwd", k, a), k)

        def left(self, d, h, a, name, k):
            if self.detour and k == 1:
                @pl.when(inner_plane)
                def _():
                    departed(self.pick(d, h, a), name)
            else:
                departed(self.pick(d, h, a), name)

        def drain(self):
            for a in range(2):
                for h, k in ((0, 1), (1, -1), (1, 1), (0, -1)):
                    self.left(0, h, a, (self.tag, "own", k, h, a), k)
                for k, h in ((1, 0), (-1, 1)):
                    self.left(-k, h, a, (self.tag, "fwd", k, a), k)
                if self.detour:
                    @pl.when(z == 1)
                    def _():
                        for d, h, name in (
                            (-1, 0, (self.tag, "own", 1, 0, a)),
                            (-1, 1, (self.tag, "own", 1, 1, a)),
                            (2, 0, (self.tag, "fwd", 1, a)),
                        ):
                            departed(self.pick(d, h, a), ("detour",) + name)

    plans = []
    for cc, mid, mid_devs, last, last_devs, other in (
        (0, mid_y, dev_y, last_x, dev_x, last_y),
        (1, mid_x, dev_x, last_y, dev_y, last_x),
    ):
        plans.append((
            Ring(mid, mid_devs, "mid", detour=DETOUR and cc == 0),
            Ring(functools.partial(last, cc), last_devs, "last", detour=DETOUR and cc == 1),
            functools.partial(last, cc),
            functools.partial(other, 1 - cc),
            cc,
        ))

    def per_core(body):
        for plan in plans:
            @pl.when(c == plan[4])
            def _():
                body(*plan)

    def share(give, cc, a, *ds):
        for d in ds:
            push(give(d, None, a), give(d, None, a), ("core", d, a, cc), dev_c)

    def first(mid, last, give, take, cc):
        end_z("zq", piece_q)
        mid.begin(0)
        end_z("zs", piece_s)
        mid.forward(0)
        mid.begin(1)
        mid.near(0)
        mid.far(0)
        last.begin(0)
        share(give, cc, 0, 0)

    def first_rest(mid, last, give, take, cc):
        mid.forward(1)
        mid.near(1)
        mid.far(1)
        last.forward(0)
        last.begin(1)
        share(give, cc, 1, 0)

    def second(mid, last, give, take, cc):
        last.near(0)
        share(give, cc, 0, -1, 1)
        last.far(0)
        share(give, cc, 0, 2)
        for d in (0, -1, 1, 2):
            arrived(take(d, None, 0), ("core", d, 0, 1 - cc))

    def third(mid, last, give, take, cc):
        last.forward(1)

    def fourth(mid, last, give, take, cc):
        last.near(1)
        share(give, cc, 1, -1, 1)

    def fifth(mid, last, give, take, cc):
        last.far(1)
        share(give, cc, 1, 2)
        for d in (0, -1, 1, 2):
            arrived(take(d, None, 1), ("core", d, 1, 1 - cc))

    def drain(mid, last, give, take, cc):
        mid.drain()
        last.drain()
        for a in range(2):
            for d in (0, -1, 1, 2):
                departed(give(d, None, a), ("core", d, a, cc))

    def weight(tile):
        g = tile // 3
        return wq[lax.rem(g, 2), g // 2, lax.rem(tile, 3)]

    def columns(head):
        return jnp.concatenate([weight(2 * head), weight(2 * head + 1)], axis=1)

    def dot(a, b):
        return jnp.dot(a, b, preferred_element_type=f32)

    def rotated(v, j, lo=0):
        n = v.shape[0]
        first_half = v[:, :128]
        swapped = jnp.where(
            lane[:n] < 32, pltpu.roll(first_half, 96, 1), pltpu.roll(first_half, 32, 1)
        )
        turned = first_half * ctab[j, lo : lo + n, :] + swapped * stab[j, lo : lo + n, :]
        return jnp.concatenate([turned, v[:, 128:]], axis=1)

    def each_head(body):
        pl.loop(0, HEADS)(body)

    def keys(j, lo=0, n=TOK):
        @each_head
        def _(h):
            kbuf[j % 2, h, lo : lo + n, :] = rotated(
                dot(H[j, lo : lo + n, :], columns(HEADS + h)), j, lo
            ).astype(bf16)

    def value_base(j):
        @each_head
        def _(h):
            vpre[j, h] = dot(H[j], columns(2 * HEADS + h))

    def query_base():
        @each_head
        def _(h):
            acc[h] = dot(H[0], columns(h))

    def ranks(j, lo=0, n=TOK):
        r = lax.dot_general(
            H[j, lo : lo + n, :], dsel[...], (((1,), (1,)), ((), ())), preferred_element_type=f32
        )
        column = lax.broadcasted_iota(i32, (n, 256), 1) // 16
        request = jnp.concatenate([owner[j, lo : lo + n, :]] * 2, axis=1)
        rbuf[lo : lo + n, :] = jnp.where(column == request, r, 0.0).astype(bf16)

    def delta(h, base, lo=0, n=TOK):
        u = usel[:, pl.ds(at(h * HS + base, HS), HS)]
        return adapter_scale_factor * dot(rbuf[lo : lo + n, :], u)

    def finish_query():
        @each_head
        def _(h):
            q = rotated(acc[h] + delta(h, 0), 0).astype(bf16)
            qbuf[h] = q * jnp.asarray(HS ** (-0.5), bf16)

    def values(j, lo=0, n=TOK):
        @each_head
        def _(h):
            if j < 2:
                base = vpre[j, h]
            else:
                base = dot(H[j, lo : lo + n, :], columns(2 * HEADS + h))
            vbuf[h, lo : lo + n, :] = (base + delta(h, WIDTH, lo, n)).astype(bf16)

    def attend(j, lo=0, n=TOK, last=False):
        begin = jnp.concatenate([begins[...]] * (n // 128), axis=1)
        row = lax.broadcasted_iota(i32, (TOK, n), 0) + s * TOK
        col = lax.broadcasted_iota(i32, (TOK, n), 1) + ((s - j) * TOK + lo)
        bias[:, :n] = jnp.where((col >= begin) & (col <= row), 0.0, -1e30).astype(f32)

        def piece(h, r):
            scores = lax.dot_general(
                qbuf[h, r, :], kbuf[j % 2, h, lo : lo + n, :], (((1,), (1,)), ((), ())),
                preferred_element_type=f32,
            ) + bias[r, :n]
            top = jnp.max(scores, axis=-1, keepdims=True)
            if j == 0:
                p = jnp.exp(scores - top)
                total = jnp.sum(p, axis=-1, keepdims=True)
                mixed = dot(p.astype(bf16), vbuf[h, lo : lo + n, :])
            else:
                before = mbuf[h, r, :][:, :1]
                top = jnp.maximum(top, before)
                fade = jnp.exp(before - top)
                p = jnp.exp(scores - top)
                total = fade * lbuf[h, r, :][:, :1] + jnp.sum(p, axis=-1, keepdims=True)
                mixed = fade * acc[h, r, :] + dot(p.astype(bf16), vbuf[h, lo : lo + n, :])
            if last:
                att[r, pl.ds(at(h * HS, HS), HS)] = (mixed / total).astype(bf16)
            else:
                acc[h, r, :] = mixed
                mbuf[h, r, :] = jnp.broadcast_to(top, (256, 128))
                lbuf[h, r, :] = jnp.broadcast_to(total, (256, 128))

        @pl.loop(0, HEADS // HEADS_AT_ONCE)
        def _(i):
            for o in range(HEADS_AT_ONCE):
                for k in range(2):
                    piece(i * HEADS_AT_ONCE + o, slice(k * 256, (k + 1) * 256))

    per_core(first)
    hop(1)
    per_core(first_rest)
    per_core(second)
    keys(0)
    query_base()
    per_core(third)
    @pl.when(z == 0)
    def _():
        hop(2)

    value_base(0)
    keys(1)
    per_core(fourth)
    value_base(1)

    @pl.when(z != 0)
    def _():
        hop(2)

    per_core(fifth)

    table = slots[...].astype(f32)
    at_slot = lax.broadcasted_iota(i32, (1, 64), 1)
    inner = lax.broadcasted_iota(i32, (16, 1024), 0)
    column = lax.broadcasted_iota(i32, (16, 1024), 1)
    for r in range(REQS):
        slot = jnp.sum(jnp.where(at_slot == ids[f, r], table, 0.0), axis=-1, keepdims=True)
        hit = column == slot.astype(i32) * 16 + inner
        onehot[r * 16 : (r + 1) * 16, :] = jnp.where(hit, 1.0, 0.0).astype(bf16)

    for g in range(8):
        for n, picked in ((1, dsel), (2, usel)):
            picked[:, g * 256 : (g + 1) * 256] = jnp.dot(
                onehot[...], ws[g % 2, g // 2, n], preferred_element_type=f32
            ).astype(bf16)

    ranks(0)
    finish_query()
    values(0)
    attend(0)
    ranks(1)
    values(1)
    attend(1)
    keys(2)
    ranks(2)
    values(2)
    attend(2)
    for k in range(2):
        arrived(part(3, k), ("halo", 2, k))
        keys(3, k * half, half)
        ranks(3, k * half, half)
        values(3, k * half, half)
        attend(3, k * half, half, last=k == 1)

    def store(g):
        return pltpu.make_async_copy(obuf.at[g % 2], out.at[:, pl.ds(g * 256, 256)], osem.at[g % 2])

    for g in range(8):
        if g >= 2:
            store(g - 2).wait()
        obuf[g % 2] = dot(att[...], ws[g % 2, g // 2, 0]).astype(bf16)
        store(g).start()
    for g in (6, 7):
        store(g).wait()

    for n in range(SPAN):
        for k in range(2):
            departed(part(n, k), ("halo", n, k))
    for k in range(NZ - 1):
        departed(piece_q(k), ("zq", k))
        departed(piece_s(k), ("zs", k))
    per_core(drain)


def run_whole(lengths, ids, slots, inverse, tokens, qkv_weight, out_weight, down, up):
    anywhere = pl.BlockSpec(memory_space=pl.ANY)
    scalar = pl.BlockSpec(memory_space=pltpu.SMEM)
    return pl.pallas_call(
        whole_kernel,
        out_shape=jax.ShapeDtypeStruct((TOK, 2 * WIDTH), bf16),
        in_specs=[scalar] * 2 + [pl.BlockSpec(memory_space=pltpu.VMEM)] * 2 + [anywhere] * 5,
        out_specs=anywhere,
        scratch_shapes=[
            pltpu.VMEM((2, NX, 3, 2048, 128), bf16),
            pltpu.VMEM((2, NX, 3, 1024, 256), bf16),
            pltpu.VMEM((SPAN + 1, TOK, 2048), bf16),
            pltpu.VMEM((2, HEADS, TOK, HS), bf16),
            pltpu.VMEM((HEADS, TOK, HS), bf16),
            pltpu.VMEM((HEADS, TOK, HS), bf16),
            pltpu.VMEM((256, 1024), bf16),
            pltpu.VMEM((256, 2048), bf16),
            pltpu.VMEM((256, 2048), bf16),
            pltpu.VMEM((TOK, 256), bf16),
            pltpu.VMEM((HEADS, TOK, HS), f32),
            pltpu.VMEM((2, HEADS, TOK, HS), f32),
            pltpu.VMEM((HEADS, TOK, 128), f32),
            pltpu.VMEM((HEADS, TOK, 128), f32),
            pltpu.VMEM((SPAN + 1, TOK, 128), f32),
            pltpu.VMEM((SPAN + 1, TOK, 128), f32),
            pltpu.VMEM((TOK, 128), i32),
            pltpu.VMEM((SPAN + 1, TOK, 128), i32),
            pltpu.VMEM((TOK, TOK), f32),
            pltpu.VMEM((2, TOK, 256), bf16),
            pltpu.VMEM((TOK, WIDTH), bf16),
            pltpu.SemaphoreType.DMA((130,)),
            pltpu.SemaphoreType.DMA((130,)),
            pltpu.SemaphoreType.DMA((8,)),
            pltpu.SemaphoreType.DMA((2,)),
        ],
        compiler_params=pltpu.CompilerParams(
            collective_id=0, has_side_effects=True, vmem_limit_bytes=63 * 1024 * 1024
        ),
    )(lengths, ids, slots, inverse, tokens, qkv_weight, out_weight, down, up)


def per_device(
    tokens, qkv_weight, out_weight, adapter_down, adapter_up, lengths, adapter_ids, adapter_slot
):
    rotary = HS // 4
    inverse = 10000.0 ** (-2.0 * (np.arange(128) % (rotary // 2)) / rotary)
    inverse = jnp.asarray(np.tile(inverse[None, :], (8, 1)), f32)
    return run_whole(
        lengths, adapter_ids, adapter_slot.reshape(1, -1), inverse, tokens, qkv_weight, out_weight,
        adapter_down.reshape(-1, 2048), adapter_up.reshape(-1, 2048),
    )


def solution(mesh):
    in_specs = (
        P(("fsdp", "seq"), None),
        P("seq", "fsdp"),
        P("seq", "fsdp"),
        P("seq", None, None),
        P("seq", None, None),
        P(),
        P(),
        P(),
    )
    out_specs = P(("fsdp", "seq"), None)
    return jax.shard_map(
        per_device, mesh=mesh, in_specs=in_specs, out_specs=out_specs, check_vma=False
    )
```

time: 217 us -> 175 us (0.81)
  the two profiles are of different devices: /device:TPU:1 before, /device:TPU:8 now
where the time goes in v3:
time: 175 us; the launch traced here: 173 us
  Pallas kernels  170 us (97%)
  local copies, waits for them, and re-layouts  3.16 us (2%)
    pallas_call x1, Pallas kernels, run_whole(): pl.pallas_call(whole_kernel, out_shape=jax.ShapeDtypeStruct((TOK, 2 * WID...  170 us

profile of v3, /device:TPU:8, one launch (start us, length us, event | category | flops | bytes accessed | tf_op | source)
XLA Modules:
  0.0 173.3 jit_solution(13441729871747628410)
XLA Ops:
  0.0 170.1 %shard_map.91 = bf16[512,2048]{1,0:T(8,128)(2,1)} custom-call(s32[8,16]{1,0:T(8,128)} %lengths.1, s32[8,16]{1,0:T(8,128)} %ids.1, s32[1,64]{1,0:T(1,128)} %bitcast.5, f32[8,128]{1,0:T(8,128)} %constant.2.clone.inverse, bf16[512,2048]{1,0:T(8,128)(2,1)} %tokens.1, bf16[64,384]{1,0:T(8,128)(2,1)} %qkv.1, bf16[32,256]{1,0:T(8,128)(2,1)} %outw.1, ...), custom_call_target="tpu_custom_call" | custom-call | tf_op jit(solution)/shard_map/pallas_call | solution.py:509
  170.1 3.2 %copy.11 = bf16[512,2048]{1,0:T(8,128)(2,1)} copy(bf16[512,2048]{1,0:T(8,128)(2,1)} %shard_map.91) | data formatting | bytes 4194304

commit v4 on v3

--- a/solution.py
+++ b/solution.py
@@ -16,7 +16,8 @@
 WIDTH = 1024
 NX, NY, NZ = 4, 4, 8
 MESH = pl.DeviceIdType.MESH
-HEADS_AT_ONCE = 1
+HEADS_AT_ONCE = 2
+OUT_AT_ONCE = 2
 DETOUR = True
 bf16, f32, i32 = jnp.bfloat16, jnp.float32, jnp.int32
 
@@ -59,6 +60,8 @@
     def piece_s(d):
         return ws.at[c, x, :, pl.ds(s_piece[d], 32), :]
 
+    parts = {1: pl.ds(1, 2), 2: pl.ds(0, 1)}
+
     own = [
         pltpu.make_async_copy(outw, piece_s(0).at[0], local.at[0]),
         pltpu.make_async_copy(down.at[:, cols], piece_s(0).at[1], local.at[1]),
@@ -177,22 +180,23 @@
     def mid_y(d, h, a):
         if a == 0:
             return wq.at[c, x, :, pl.ds(q_rows[d][h], 256), :]
-        return ws.at[c, x, :, pl.ds(s_rows[d][h], 128), :]
+        return ws.at[c, x, parts[a], pl.ds(s_rows[d][h], 128), :]
 
     def mid_x(d, h, a):
         if a == 0:
             return wq.at[c, xs[d], :, pl.ds(q_rows[0][h], 256), :]
-        return ws.at[c, xs[d], :, pl.ds(s_rows[0][h], 128), :]
+        return ws.at[c, xs[d], parts[a], pl.ds(s_rows[0][h], 128), :]
 
     def last_x(cc, d, h, a):
         if a == 0:
             return wq.at[cc, xs[d]] if h is None else wq.at[cc, xs[d], :, pl.ds(h * 1024, 1024), :]
-        return ws.at[cc, xs[d]] if h is None else ws.at[cc, xs[d], :, pl.ds(h * 512, 512), :]
+        base, size = (0, 1024) if h is None else (h * 512, 512)
+        return ws.at[cc, xs[d], parts[a], pl.ds(base, size), :]
 
     def last_y(cc, d, h, a):
         if a == 0:
             return wq.at[cc, :, :, pl.ds(q_rows[d][h], 512 if h is None else 256), :]
-        return ws.at[cc, :, :, pl.ds(s_rows[d][h], 256 if h is None else 128), :]
+        return ws.at[cc, :, parts[a], pl.ds(s_rows[d][h], 256 if h is None else 128), :]
 
     inner_plane = z != 0
 
@@ -241,7 +245,7 @@
                 departed(self.pick(d, h, a), name)
 
         def drain(self):
-            for a in range(2):
+            for a in range(3):
                 for h, k in ((0, 1), (1, -1), (1, 1), (0, -1)):
                     self.left(0, h, a, (self.tag, "own", k, h, a), k)
                 for k, h in ((1, 0), (-1, 1)):
@@ -292,22 +296,31 @@
 
     def first_rest(mid, last, give, take, cc):
         mid.forward(1)
+        mid.begin(2)
         mid.near(1)
         mid.far(1)
         last.forward(0)
         last.begin(1)
         share(give, cc, 1, 0)
+        mid.forward(2)
 
     def second(mid, last, give, take, cc):
         last.near(0)
         share(give, cc, 0, -1, 1)
+        mid.near(2)
+        mid.far(2)
         last.far(0)
         share(give, cc, 0, 2)
+        receive(take, cc, 0)
+
+    def receive(take, cc, a):
         for d in (0, -1, 1, 2):
-            arrived(take(d, None, 0), ("core", d, 0, 1 - cc))
+            arrived(take(d, None, a), ("core", d, a, 1 - cc))
 
     def third(mid, last, give, take, cc):
         last.forward(1)
+        last.begin(2)
+        share(give, cc, 2, 0)
 
     def fourth(mid, last, give, take, cc):
         last.near(1)
@@ -316,13 +329,26 @@
     def fifth(mid, last, give, take, cc):
         last.far(1)
         share(give, cc, 1, 2)
-        for d in (0, -1, 1, 2):
-            arrived(take(d, None, 1), ("core", d, 1, 1 - cc))
+        receive(take, cc, 1)
+
+    def out_second(mid, last, give, take, cc):
+        last.forward(2)
+
+    def out_third(mid, last, give, take, cc):
+        last.near(2)
+        share(give, cc, 2, -1, 1)
+
+    def out_last(mid, last, give, take, cc):
+        last.far(2)
+        share(give, cc, 2, 2)
+
+    def out_received(mid, last, give, take, cc):
+        receive(take, cc, 2)
 
     def drain(mid, last, give, take, cc):
         mid.drain()
         last.drain()
-        for a in range(2):
+        for a in range(3):
             for d in (0, -1, 1, 2):
                 departed(give(d, None, a), ("core", d, a, cc))
 
@@ -392,41 +418,58 @@
                 base = dot(H[j, lo : lo + n, :], columns(2 * HEADS + h))
             vbuf[h, lo : lo + n, :] = (base + delta(h, WIDTH, lo, n)).astype(bf16)
 
-    def attend(j, lo=0, n=TOK, last=False):
+    def set_bias(j, lo, n):
         begin = jnp.concatenate([begins[...]] * (n // 128), axis=1)
         row = lax.broadcasted_iota(i32, (TOK, n), 0) + s * TOK
         col = lax.broadcasted_iota(i32, (TOK, n), 1) + ((s - j) * TOK + lo)
         bias[:, :n] = jnp.where((col >= begin) & (col <= row), 0.0, -1e30).astype(f32)
 
-        def piece(h, r):
-            scores = lax.dot_general(
-                qbuf[h, r, :], kbuf[j % 2, h, lo : lo + n, :], (((1,), (1,)), ((), ())),
-                preferred_element_type=f32,
-            ) + bias[r, :n]
-            top = jnp.max(scores, axis=-1, keepdims=True)
-            if j == 0:
-                p = jnp.exp(scores - top)
-                total = jnp.sum(p, axis=-1, keepdims=True)
-                mixed = dot(p.astype(bf16), vbuf[h, lo : lo + n, :])
-            else:
-                before = mbuf[h, r, :][:, :1]
-                top = jnp.maximum(top, before)
-                fade = jnp.exp(before - top)
-                p = jnp.exp(scores - top)
-                total = fade * lbuf[h, r, :][:, :1] + jnp.sum(p, axis=-1, keepdims=True)
-                mixed = fade * acc[h, r, :] + dot(p.astype(bf16), vbuf[h, lo : lo + n, :])
-            if last:
-                att[r, pl.ds(at(h * HS, HS), HS)] = (mixed / total).astype(bf16)
-            else:
-                acc[h, r, :] = mixed
-                mbuf[h, r, :] = jnp.broadcast_to(top, (256, 128))
-                lbuf[h, r, :] = jnp.broadcast_to(total, (256, 128))
+    def soften(h, r, key, value, first=False, last=False):
+        scores = lax.dot_general(
+            qbuf[h, r, :], key, (((1,), (1,)), ((), ())), preferred_element_type=f32
+        ) + bias[r, : key.shape[0]]
+        top = jnp.max(scores, axis=-1, keepdims=True)
+        if first:
+            p = jnp.exp(scores - top)
+            total = jnp.sum(p, axis=-1, keepdims=True)
+            mixed = dot(p.astype(bf16), value)
+        else:
+            before = mbuf[h, r, :][:, :1]
+            top = jnp.maximum(top, before)
+            fade = jnp.exp(before - top)
+            p = jnp.exp(scores - top)
+            total = fade * lbuf[h, r, :][:, :1] + jnp.sum(p, axis=-1, keepdims=True)
+            mixed = fade * acc[h, r, :] + dot(p.astype(bf16), value)
+        if last:
+            att[r, pl.ds(at(h * HS, HS), HS)] = (mixed / total).astype(bf16)
+        else:
+            acc[h, r, :] = mixed
+            mbuf[h, r, :] = jnp.broadcast_to(top, (256, 128))
+            lbuf[h, r, :] = jnp.broadcast_to(total, (256, 128))
+
+    tiles = (slice(0, 256), slice(256, 512))
+
+    def attend(j):
+        set_bias(j, 0, TOK)
+
+        @each_head
+        def _(h):
+            for r in tiles:
+                soften(h, r, kbuf[j % 2, h], vbuf[h], first=j == 0)
+
+    def project_and_attend(j, lo, n, last):
+        set_bias(j, lo, n)
+        ranks(j, lo, n)
 
         @pl.loop(0, HEADS // HEADS_AT_ONCE)
         def _(i):
             for o in range(HEADS_AT_ONCE):
-                for k in range(2):
-                    piece(i * HEADS_AT_ONCE + o, slice(k * 256, (k + 1) * 256))
+                h = i * HEADS_AT_ONCE + o
+                rows = H[j, lo : lo + n, :]
+                key = rotated(dot(rows, columns(HEADS + h)), j, lo).astype(bf16)
+                value = (dot(rows, columns(2 * HEADS + h)) + delta(h, WIDTH, lo, n)).astype(bf16)
+                for r in tiles:
+                    soften(h, r, key, value, last=last)
 
     per_core(first)
     hop(1)
@@ -449,6 +492,7 @@
         hop(2)
 
     per_core(fifth)
+    per_core(out_second)
 
     table = slots[...].astype(f32)
     at_slot = lax.broadcasted_iota(i32, (1, 64), 1)
@@ -469,29 +513,34 @@
     finish_query()
     values(0)
     attend(0)
+    per_core(out_third)
     ranks(1)
     values(1)
     attend(1)
+    per_core(out_last)
     keys(2)
     ranks(2)
     values(2)
     attend(2)
+    per_core(out_received)
     for k in range(2):
         arrived(part(3, k), ("halo", 2, k))
-        keys(3, k * half, half)
-        ranks(3, k * half, half)
-        values(3, k * half, half)
-        attend(3, k * half, half, last=k == 1)
+        project_and_attend(3, k * half, half, last=k == 1)
 
     def store(g):
-        return pltpu.make_async_copy(obuf.at[g % 2], out.at[:, pl.ds(g * 256, 256)], osem.at[g % 2])
+        part_of = pl.ds(at(g * 256, 256), 256)
+        return pltpu.make_async_copy(obuf.at[:, part_of], out.at[:, part_of], osem.at[g])
+
+    @pl.loop(0, 8 // OUT_AT_ONCE)
+    def _(i):
+        for o in range(OUT_AT_ONCE):
+            g = i * OUT_AT_ONCE + o
+            obuf[:, pl.ds(at(g * 256, 256), 256)] = dot(
+                att[...], ws[lax.rem(g, 2), g // 2, 0]
+            ).astype(bf16)
+            store(g).start()
 
     for g in range(8):
-        if g >= 2:
-            store(g - 2).wait()
-        obuf[g % 2] = dot(att[...], ws[g % 2, g // 2, 0]).astype(bf16)
-        store(g).start()
-    for g in (6, 7):
         store(g).wait()
 
     for n in range(SPAN):
@@ -531,12 +580,12 @@
             pltpu.VMEM((TOK, 128), i32),
             pltpu.VMEM((SPAN + 1, TOK, 128), i32),
             pltpu.VMEM((TOK, TOK), f32),
-            pltpu.VMEM((2, TOK, 256), bf16),
+            pltpu.VMEM((TOK, 2 * WIDTH), bf16),
             pltpu.VMEM((TOK, WIDTH), bf16),
-            pltpu.SemaphoreType.DMA((130,)),
-            pltpu.SemaphoreType.DMA((130,)),
+            pltpu.SemaphoreType.DMA((190,)),
+            pltpu.SemaphoreType.DMA((190,)),
             pltpu.SemaphoreType.DMA((8,)),
-            pltpu.SemaphoreType.DMA((2,)),
+            pltpu.SemaphoreType.DMA((8,)),
         ],
         compiler_params=pltpu.CompilerParams(
             collective_id=0, has_side_effects=True, vmem_limit_bytes=63 * 1024 * 1024

time: 175 us -> 165 us (0.943)
  Pallas kernels: 170 us -> 159 us
    pallas_call x1, Pallas kernels: 170 us -> 159 us  [run_whole(): pl.pallas_call(whole_kernel, out_shape=jax.ShapeDtypeStruct((TOK, 2 * WID...]
where the time goes in v4:
time: 165 us; the launch traced here: 162 us
  Pallas kernels  159 us (96%)
  local copies, waits for them, and re-layouts  3.16 us (2%)
    pallas_call x1, Pallas kernels, run_whole(): pl.pallas_call(whole_kernel, out_shape=jax.ShapeDtypeStruct((TOK, 2 * WID...  159 us

profile of v4, /device:TPU:8, one launch (start us, length us, event | category | flops | bytes accessed | tf_op | source)
XLA Modules:
  0.0 162.2 jit_solution(6097004656929018580)
XLA Ops:
  0.0 159.0 %shard_map.91 = bf16[512,2048]{1,0:T(8,128)(2,1)} custom-call(s32[8,16]{1,0:T(8,128)} %lengths.1, s32[8,16]{1,0:T(8,128)} %ids.1, s32[1,64]{1,0:T(1,128)} %bitcast.5, f32[8,128]{1,0:T(8,128)} %constant.2.clone.inverse, bf16[512,2048]{1,0:T(8,128)(2,1)} %tokens.1, bf16[64,384]{1,0:T(8,128)(2,1)} %qkv.1, bf16[32,256]{1,0:T(8,128)(2,1)} %outw.1, ...), custom_call_target="tpu_custom_call" | custom-call | tf_op jit(solution)/shard_map/pallas_call | solution.py:558
  159.0 3.2 %copy.11 = bf16[512,2048]{1,0:T(8,128)(2,1)} copy(bf16[512,2048]{1,0:T(8,128)(2,1)} %shard_map.91) | data formatting | bytes 4194304

commit v5 on v4

--- a/solution.py
+++ b/solution.py
@@ -17,6 +17,7 @@
 NX, NY, NZ = 4, 4, 8
 MESH = pl.DeviceIdType.MESH
 HEADS_AT_ONCE = 2
+PARTS = 2
 OUT_AT_ONCE = 2
 DETOUR = True
 bf16, f32, i32 = jnp.bfloat16, jnp.float32, jnp.int32
@@ -110,26 +111,25 @@
             device_id=self_id, device_id_type=MESH,
         ).wait_send()
 
-    half = TOK // 2
+    size = TOK // PARTS
 
     def part(n, k):
-        return H.at[n, pl.ds(k * half, half), :]
+        return H.at[n, pl.ds(k * size, size), :]
 
     def hop_part(n, k):
         push(part(n, k), part(n + 1, k), ("halo", n, k), following)
 
-    def hop(n):
-        for k in range(2):
-            arrived(part(n, k), ("halo", n - 1, k))
-            hop_part(n, k)
+    def hop(n, k):
+        arrived(part(n, k), ("halo", n - 1, k))
+        hop_part(n, k)
 
     lane = lax.broadcasted_iota(i32, (TOK, 128), 1)
     token = lax.broadcasted_iota(i32, (TOK, 128), 0)
 
     def norm(k):
-        @pl.loop(0, half // 64)
+        @pl.loop(0, size // 64)
         def _(i):
-            r = pl.ds(at(k * half + i * 64, 64), 64)
+            r = pl.ds(at(k * size + i * 64, 64), 64)
             v = H[0, r, :].astype(f32)
             mean = jnp.mean(v, axis=-1, keepdims=True)
             centred = v - mean
@@ -166,12 +166,12 @@
     for copy in own:
         copy.wait()
     z_step(0)
-    norm(1)
-    hop_part(0, 1)
-    z_step(1)
-    for k in range(2, NZ - 1):
+    for k in range(1, PARTS):
+        norm(k)
+        hop_part(0, k)
+    for k in range(1, NZ - 1):
         z_step(k)
-        if k - 2 <= SPAN:
+        if 0 <= k - 2 <= SPAN:
             tables(k - 2)
 
     def end_z(name, piece):
@@ -472,25 +472,19 @@
                     soften(h, r, key, value, last=last)
 
     per_core(first)
-    hop(1)
+    hop(1, 0)
     per_core(first_rest)
+    hop(1, 1)
     per_core(second)
     keys(0)
     query_base()
     per_core(third)
-    @pl.when(z == 0)
-    def _():
-        hop(2)
-
+    hop(2, 0)
     value_base(0)
     keys(1)
     per_core(fourth)
     value_base(1)
-
-    @pl.when(z != 0)
-    def _():
-        hop(2)
-
+    hop(2, 1)
     per_core(fifth)
     per_core(out_second)
 
@@ -523,9 +517,10 @@
     values(2)
     attend(2)
     per_core(out_received)
-    for k in range(2):
-        arrived(part(3, k), ("halo", 2, k))
-        project_and_attend(3, k * half, half, last=k == 1)
+    for ks in ((0,), (1,)):
+        for k in ks:
+            arrived(part(3, k), ("halo", 2, k))
+        project_and_attend(3, ks[0] * size, len(ks) * size, last=ks[-1] == PARTS - 1)
 
     def store(g):
         part_of = pl.ds(at(g * 256, 256), 256)
@@ -543,13 +538,16 @@
     for g in range(8):
         store(g).wait()
 
-    for n in range(SPAN):
-        for k in range(2):
+    for n in range(SPAN - 1):
+        for k in range(PARTS):
             departed(part(n, k), ("halo", n, k))
     for k in range(NZ - 1):
         departed(piece_q(k), ("zq", k))
         departed(piece_s(k), ("zs", k))
     per_core(drain)
+
+    for k in range(PARTS):
+        departed(part(SPAN - 1, k), ("halo", SPAN - 1, k))
 
 
 def run_whole(lengths, ids, slots, inverse, tokens, qkv_weight, out_weight, down, up):
@@ -582,8 +580,8 @@
             pltpu.VMEM((TOK, TOK), f32),
             pltpu.VMEM((TOK, 2 * WIDTH), bf16),
             pltpu.VMEM((TOK, WIDTH), bf16),
-            pltpu.SemaphoreType.DMA((190,)),
-            pltpu.SemaphoreType.DMA((190,)),
+            pltpu.SemaphoreType.DMA((200,)),
+            pltpu.SemaphoreType.DMA((200,)),
             pltpu.SemaphoreType.DMA((8,)),
             pltpu.SemaphoreType.DMA((8,)),
         ],

time: 165 us -> 165 us (level)
  no operation moved by 1% of the time
where the time goes in v5:
time: 165 us; the launch traced here: 162 us
  Pallas kernels  159 us (96%)
  local copies, waits for them, and re-layouts  3.16 us (2%)
    pallas_call x1, Pallas kernels, run_whole(): pl.pallas_call(whole_kernel, out_shape=jax.ShapeDtypeStruct((TOK, 2 * WID...  159 us

profile of v5, /device:TPU:8, one launch (start us, length us, event | category | flops | bytes accessed | tf_op | source)
XLA Modules:
  0.0 162.4 jit_solution(13823070766045195302)
XLA Ops:
  0.0 159.2 %shard_map.91 = bf16[512,2048]{1,0:T(8,128)(2,1)} custom-call(s32[8,16]{1,0:T(8,128)} %lengths.1, s32[8,16]{1,0:T(8,128)} %ids.1, s32[1,64]{1,0:T(1,128)} %bitcast.5, f32[8,128]{1,0:T(8,128)} %constant.2.clone.inverse, bf16[512,2048]{1,0:T(8,128)(2,1)} %tokens.1, bf16[64,384]{1,0:T(8,128)(2,1)} %qkv.1, bf16[32,256]{1,0:T(8,128)(2,1)} %outw.1, ...), custom_call_target="tpu_custom_call" | custom-call | tf_op jit(solution)/shard_map/pallas_call | solution.py:556
  159.2 3.2 %copy.11 = bf16[512,2048]{1,0:T(8,128)(2,1)} copy(bf16[512,2048]{1,0:T(8,128)(2,1)} %shard_map.91) | data formatting | bytes 4194304
